TPU v7x, 128 devices: a whole 4x4x4 slice. The times are simulated.
128 devices in a mesh: smp: 8 (over y, core), gx: 8 (over z_lo, x), gz: 2 (over z_hi).
Axes of the slice: x: 4, y: 4, z: 4 (z_hi: 2, z_lo: 2; z = z_hi * 2 + z_lo), core: 2. Of those that a mesh axis runs over, the one named last changes fastest.
Arguments:
- features: bfloat16 [8, 32, 40, 8, 256], P('smp', None, 'gx', None, 'gz'), may hold values from -6 to 6
- first_weight: bfloat16 [32, 3, 3, 3, 32], replicated, may hold values from -0.21875 to 0.21875
- first_bias: float32 [32], replicated, may hold values from -1 to 1
- second_weight: bfloat16 [32, 3, 3, 3, 32], replicated, may hold values from -0.21875 to 0.21875
- second_bias: float32 [32], replicated, may hold values from -1 to 1
- cotangent: bfloat16 [8, 32, 40, 8, 256], P('smp', None, 'gx', None, 'gz'), may hold values from -6 to 6
Outputs:
- output: bfloat16 [8, 32, 40, 8, 256], P('smp', None, 'gx', None, 'gz')
- first_grad: float32 [32, 3, 3, 3, 32], replicated
- first_bias_grad: float32 [32], replicated
- second_grad: float32 [32, 3, 3, 3, 32], replicated
- second_bias_grad: float32 [32], replicated
All inputs are finite; a program needn't handle non-finite values.
Results may differ from a plain program's by a relative error of at most 0.011.
Values may be sent and summed in bfloat16 or wider, within the bound.
A program may use at most 128 MiB of HBM per device.

v0:
```python
import jax
import jax.numpy as jnp
from jax import lax
from jax.sharding import PartitionSpec as P


def extended(array, sides, width):
    for axis, dim in sides:
        size, length = (lax.axis_size(axis), array.shape[dim])
        up = [(i, (i + 1) % size) for i in range(size)]
        down = [(j, i) for i, j in up]
        last = lax.slice_in_dim(array, length - width, length, axis=dim)
        initial = lax.slice_in_dim(array, 0, width, axis=dim)
        before = lax.ppermute(last, axis, up)
        after = lax.ppermute(initial, axis, down)
        array = jnp.concatenate([before, array, after], axis=dim)
    return array


def wall_pad(field_in):
    return jnp.pad(field_in, ((0, 0), (0, 0), (0, 0), (1, 1), (0, 0)))


def extend(field_in, depth_cells):
    both_wide = extended(field_in, (("gx", 2), ("gz", 4)), depth_cells)
    return wall_pad(both_wide)


def stack_taps(padded, offset_x, offset_y, cells_x, cells_y, cells_z):
    return jnp.concatenate(
        [
            padded[
                :,
                :,
                offset_x : offset_x + cells_x,
                offset_y : offset_y + cells_y,
                offset_z : offset_z + cells_z,
            ]
            for offset_z in range(3)
        ],
        axis=1,
    )


def convolve(padded, weight):
    cells_x = padded.shape[2] - 2
    cells_y = padded.shape[3] - 2
    cells_z = padded.shape[4] - 2
    summed = jnp.zeros((padded.shape[0], weight.shape[0], cells_x, cells_y, cells_z), jnp.float32)
    for offset_x in range(3):
        for offset_y in range(3):
            stacked = stack_taps(padded, offset_x, offset_y, cells_x, cells_y, cells_z)
            tap_block = weight[:, offset_x, offset_y].reshape(weight.shape[0], -1)
            summed = summed + jnp.einsum(
                "ok,skxyz->soxyz", tap_block, stacked, preferred_element_type=jnp.float32
            )
    return summed


def correlate(upstream, padded):
    cells_x = upstream.shape[2]
    cells_y = upstream.shape[3]
    cells_z = upstream.shape[4]
    outer_terms = []
    for offset_x in range(3):
        inner_terms = []
        for offset_y in range(3):
            stacked = stack_taps(padded, offset_x, offset_y, cells_x, cells_y, cells_z)
            local_term = jnp.einsum(
                "soxyz,skxyz->ok", upstream, stacked, preferred_element_type=jnp.float32
            )
            inner_terms.append(local_term.reshape(upstream.shape[1], 3, -1))
        outer_terms.append(jnp.stack(inner_terms, axis=1))
    return jnp.stack(outer_terms, axis=1)


def shards(features, first_weight, first_bias, second_weight, second_bias, cotangent):
    input_pad = extend(features, 1)
    preact = convolve(input_pad, first_weight) + first_bias[None, :, None, None, None]
    hidden = jax.nn.silu(preact).astype(jnp.bfloat16)
    hidden_pad = extend(hidden, 1)
    residual_term = convolve(hidden_pad, second_weight) + second_bias[None, :, None, None, None]
    output = (features.astype(jnp.float32) + residual_term).astype(jnp.bfloat16)
    cells_all = (
        features.shape[0]
        * lax.axis_size("smp")
        * features.shape[2]
        * lax.axis_size("gx")
        * features.shape[3]
        * features.shape[4]
        * lax.axis_size("gz")
    )
    grad_scale = 1.0 / cells_all**0.5
    second_grad = correlate(cotangent, hidden_pad) * grad_scale
    second_bgrad = jnp.sum(cotangent, axis=(0, 2, 3, 4), dtype=jnp.float32) * grad_scale
    flipped = jnp.transpose(jnp.flip(second_weight, (1, 2, 3)), (4, 1, 2, 3, 0))
    upstream_pad = extend(cotangent, 1)
    hidden_grad = convolve(upstream_pad, flipped)
    logistic = jax.nn.sigmoid(preact)
    preact_grad = (hidden_grad * logistic * (1.0 + preact * (1.0 - logistic))).astype(jnp.bfloat16)
    first_grad = correlate(preact_grad, input_pad) * grad_scale
    first_bgrad = jnp.sum(preact_grad, axis=(0, 2, 3, 4), dtype=jnp.float32) * grad_scale
    first_grad, first_bgrad, second_grad, second_bgrad = lax.psum(
        (first_grad, first_bgrad, second_grad, second_bgrad), ("smp", "gx", "gz")
    )
    return (output, first_grad, first_bgrad, second_grad, second_bgrad)


def solution(mesh):
    in_specs = (
        P("smp", None, "gx", None, "gz"),
        P(),
        P(),
        P(),
        P(),
        P("smp", None, "gx", None, "gz"),
    )
    out_specs = (P("smp", None, "gx", None, "gz"), P(), P(), P(), P())
    return jax.shard_map(shards, mesh=mesh, in_specs=in_specs, out_specs=out_specs, check_vma=False)
```

profile of v0, /device:TPU:1, one launch (start us, length us, event | category | flops | bytes accessed | tf_op | source)
XLA Modules:
  0.0 336.7 jit_solution(1771370892015134245)
XLA Ops:
  7.2 1.1 copy.113
  8.3 4.7 %collective-permute-start.9 = (bf16[1,32,1,8,128]{4,1,3,2,0:T(8,128)(2,1)S(1)}, bf16[1,32,1,8,128]{4,1,3,2,0:T(8,128)(2,1)S(1)}, u32[]{:S(2)}, u32[]{:S(2)}) collective-permute-start(bf16[1,32,1,8,128]{4,1,3,2,0:T(8,128)(2,1)S(1)} %get-tuple-element.105), channel_id=1, source_target_pairs={{2,0},{4,2},{6,4},{8,6},{10,8},{12,10},{14,12},{0,14},{3,1},{5,3},... | collective-permute-start | bytes 196616 | tf_op jit(solution)/shard_map/ppermute | solution.py:15
  13.1 1.1 copy.88
  14.2 3.6 %collective-permute-start.1 = (bf16[1,32,1,8,128]{4,1,3,2,0:T(8,128)(2,1)S(1)}, bf16[1,32,1,8,128]{4,1,3,2,0:T(8,128)(2,1)S(1)}, u32[]{:S(2)}, u32[]{:S(2)}) collective-permute-start(bf16[1,32,1,8,128]{4,1,3,2,0:T(8,128)(2,1)S(1)} %get-tuple-element.109), channel_id=1, source_target_pairs={{2,0},{4,2},{6,4},{8,6},{10,8},{12,10},{14,12},{0,14},{3,1},{5,3},... | collective-permute-start | bytes 196616 | tf_op jit(solution)/shard_map/ppermute | solution.py:15
  20.6 2.4 collective-permute-done
  23.1 3.4 %collective-permute-start.10 = (bf16[1,32,7,8,1]{4,1,3,2,0:T(8,128)(2,1)S(1)}, bf16[1,32,7,8,1]{4,1,3,2,0:T(8,128)(2,1)S(1)}, u32[]{:S(2)}, u32[]{:S(2)}) collective-permute-start(bf16[1,32,7,8,1]{4,1,3,2,0:T(8,128)(2,1)S(1)} %get-tuple-element.89), channel_id=1, source_target_pairs={{0,1},{1,0},{2,3},{3,2},{4,5},{5,4},{6,7},{7,6},{8,9},{9,8},{10,11... | collective-permute-start | bytes 10760 | tf_op jit(solution)/shard_map/ppermute | solution.py:14
  26.8 3.0 collective-permute-start.2
  29.8 4.7 %collective-permute-done.10 = bf16[1,32,7,8,1]{4,1,3,2,0:T(8,128)(2,1)S(1)} collective-permute-done((bf16[1,32,7,8,1]{4,1,3,2,0:T(8,128)(2,1)S(1)}, bf16[1,32,7,8,1]{4,1,3,2,0:T(8,128)(2,1)S(1)}, u32[]{:S(2)}, u32[]{:S(2)}) %collective-permute-start.10) | collective-permute-done | bytes 3616 | tf_op jit(solution)/shard_map/ppermute | solution.py:14
  34.5 9.8 %collective-permute-done.11 = bf16[1,32,7,8,1]{4,1,3,2,0:T(8,128)(2,1)S(1)} collective-permute-done((bf16[1,32,7,8,1]{4,1,3,2,0:T(8,128)(2,1)S(1)}, bf16[1,32,7,8,1]{4,1,3,2,0:T(8,128)(2,1)S(1)}, u32[]{:S(2)}, u32[]{:S(2)}) %collective-permute-start.11) | collective-permute-done | bytes 3616 | tf_op jit(solution)/shard_map/ppermute | solution.py:15
  44.9 1.5 fusion.148
  46.5 7.7 %collective-permute-done.2 = bf16[1,32,7,8,1]{4,1,3,2,0:T(8,128)(2,1)S(1)} collective-permute-done((bf16[1,32,7,8,1]{4,1,3,2,0:T(8,128)(2,1)S(1)}, bf16[1,32,7,8,1]{4,1,3,2,0:T(8,128)(2,1)S(1)}, u32[]{:S(2)}, u32[]{:S(2)}) %collective-permute-start.2) | collective-permute-done | bytes 3616 | tf_op jit(solution)/shard_map/ppermute | solution.py:14
  54.2 9.8 %collective-permute-done.3 = bf16[1,32,7,8,1]{4,1,3,2,0:T(8,128)(2,1)S(1)} collective-permute-done((bf16[1,32,7,8,1]{4,1,3,2,0:T(8,128)(2,1)S(1)}, bf16[1,32,7,8,1]{4,1,3,2,0:T(8,128)(2,1)S(1)}, u32[]{:S(2)}, u32[]{:S(2)}) %collective-permute-start.3) | collective-permute-done | bytes 3616 | tf_op jit(solution)/shard_map/ppermute | solution.py:15
  64.0 0.6 fusion.20
  64.6 1.5 fusion.150
  66.4 0.6 fusion.101
  67.1 1.1 pad_maximum_fusion.14
  71.7 0.6 fusion.97
  74.2 1.0 convolution_add_fusion.1
  75.9 0.7 convolution_bitcast_fusion.6
  76.6 0.7 convolution_bitcast_fusion.5
  77.3 0.7 convolution_bitcast_fusion.4
  78.0 0.7 convolution_bitcast_fusion.3
  78.7 0.7 convolution_bitcast_fusion.1
  79.4 0.7 convolution_bitcast_fusion.7
  80.1 0.7 convolution_bitcast_fusion.8
  80.9 0.7 convolution_bitcast_fusion.2
  81.6 0.7 convolution_bitcast_fusion
  82.4 3.6 %collective-permute-start.5 = (bf16[1,32,1,8,128]{4,1,3,2,0:T(8,128)(2,1)S(1)}, bf16[1,32,1,8,128]{4,1,3,2,0:T(8,128)(2,1)S(1)}, u32[]{:S(2)}, u32[]{:S(2)}) collective-permute-start(bf16[1,32,1,8,128]{4,1,3,2,0:T(8,128)(2,1)S(1)} %get-tuple-element.108), channel_id=1, source_target_pairs={{2,0},{4,2},{6,4},{8,6},{10,8},{12,10},{14,12},{0,14},{3,1},{5,3},... | collective-permute-start | bytes 196616 | tf_op jit(solution)/shard_map/ppermute | solution.py:15
  86.0 1.6 collective-permute-done.4
  87.9 2.8 collective-permute-start.6
  91.0 0.8 maximum_multiply_fusion
  91.8 78.4 %all-reduce.3 = (f32[32]{0:T(128)}, f32[32]{0:T(128)}) all-reduce(f32[32]{0:T(128)S(1)} %broadcast_multiply_fusion.1, f32[32]{0:T(128)S(1)} %broadcast_multiply_fusion), channel_id=1, replica_groups=mesh['smp'=8,'gx'=8,'gz'=2] {'smp','gx','gz'}, use_global_device_ids=true, to_apply=%region_2.3 | all-reduce | flops 64 | bytes 512 | tf_op jit(solution)/shard_map/psum | solution.py:103
  170.1 0.7 maximum_maximum_fusion
  171.7 0.7 convolution_bitcast_fusion.13
  172.4 0.7 convolution_bitcast_fusion.10
  173.1 0.7 convolution_bitcast_fusion.16
  174.4 1.4 fusion.149
  176.0 0.7 convolution_bitcast_fusion.11
  176.7 0.7 convolution_bitcast_fusion.9
  177.7 0.7 convolution_bitcast_fusion.14
  178.4 0.7 convolution_bitcast_fusion.12
  179.6 0.7 convolution_bitcast_fusion.17
  180.3 0.7 convolution_bitcast_fusion.15
  183.0 0.8 maximum_multiply_fusion.1
  184.1 0.9 copy.164
  185.0 142.2 %all-reduce.7.cloned.1.call-done = (f32[32,3,3,3,32]{4,0,3,2,1:T(8,128)}, f32[32,3,3,3,32]{4,0,3,2,1:T(8,128)}) async-done(((f32[32,3,3,3,32]{4,0,3,2,1:T(8,128)}, f32[32,3,3,3,32]{4,0,3,2,1:T(8,128)}), (f32[32,3,3,3,32]{4,0,3,2,1:T(8,128)}, f32[32,3,3,3,32]{4,0,3,2,1:T(8,128)})) %all-reduce.7.cloned.1.call-update) | async-done | bytes 221200 | tf_op jit(solution)/shard_map/psum | solution.py:103
  327.2 1.9 copy.328
  329.1 0.8 copy.329
  (126 shorter events, 15.3 us)
Async XLA Ops:
  7.2 10.6 %copy-start = (bf16[1,32,5,8,128]{4,3,2,1,0:T(8,128)(2,1)S(1)}, bf16[1,32,5,8,128]{4,3,2,1,0:T(8,128)(2,1)}, u32[]{:S(2)}) copy-start(bf16[1,32,5,8,128]{4,3,2,1,0:T(8,128)(2,1)} %param.11) | copy-start | bytes 983044
  7.2 10.9 %copy-start.2 = (bf16[32,3,3,3,32]{4,0,3,2,1:T(8,128)(2,1)S(1)}, bf16[32,3,3,3,32]{4,0,3,2,1:T(8,128)(2,1)}, u32[]{:S(2)}) copy-start(bf16[32,3,3,3,32]{4,0,3,2,1:T(8,128)(2,1)} %param.9) | copy-start | bytes 165892
  7.2 320.0 %all-reduce.7.cloned.1.call-start = ((), (), s32[]{:S(2)}) async-start(), calls=%async_computation | async-start | bytes 1769472 | tf_op jit(solution)/shard_map/psum | solution.py:103
  8.3 12.0 %collective-permute-start.9 = (bf16[1,32,1,8,128]{4,1,3,2,0:T(8,128)(2,1)S(1)}, bf16[1,32,1,8,128]{4,1,3,2,0:T(8,128)(2,1)S(1)}, u32[]{:S(2)}, u32[]{:S(2)}) collective-permute-start(bf16[1,32,1,8,128]{4,1,3,2,0:T(8,128)(2,1)S(1)} %get-tuple-element.105), channel_id=1, source_target_pairs={{2,0},{4,2},{6,4},{8,6},{10,8},{12,10},{14,12},{0,14},{3,1},{5,3},... | collective-permute-start | bytes 196616 | tf_op jit(solution)/shard_map/ppermute | solution.py:15
  13.1 5.1 %copy-start.4 = (bf16[32,3,3,3,32]{4,0,3,2,1:T(8,128)(2,1)S(1)}, bf16[32,3,3,3,32]{4,0,3,2,1:T(8,128)(2,1)}, u32[]{:S(2)}) copy-start(bf16[32,3,3,3,32]{4,0,3,2,1:T(8,128)(2,1)} %param.7) | copy-start | bytes 165892
  13.1 7.2 %collective-permute-start.8 = (bf16[1,32,1,8,128]{4,1,3,2,0:T(8,128)(2,1)S(1)}, bf16[1,32,1,8,128]{4,1,3,2,0:T(8,128)(2,1)S(1)}, u32[]{:S(2)}, u32[]{:S(2)}) collective-permute-start(bf16[1,32,1,8,128]{4,1,3,2,0:T(8,128)(2,1)S(1)} %get-tuple-element.106), channel_id=1, source_target_pairs={{0,2},{2,4},{4,6},{6,8},{8,10},{10,12},{12,14},{14,0},{1,3},{3,5},... | collective-permute-start | bytes 196616 | tf_op jit(solution)/shard_map/ppermute | solution.py:14
  14.2 12.4 %collective-permute-start.1 = (bf16[1,32,1,8,128]{4,1,3,2,0:T(8,128)(2,1)S(1)}, bf16[1,32,1,8,128]{4,1,3,2,0:T(8,128)(2,1)S(1)}, u32[]{:S(2)}, u32[]{:S(2)}) collective-permute-start(bf16[1,32,1,8,128]{4,1,3,2,0:T(8,128)(2,1)S(1)} %get-tuple-element.109), channel_id=1, source_target_pairs={{2,0},{4,2},{6,4},{8,6},{10,8},{12,10},{14,12},{0,14},{3,1},{5,3},... | collective-permute-start | bytes 196616 | tf_op jit(solution)/shard_map/ppermute | solution.py:15
  17.8 5.2 %collective-permute-start = (bf16[1,32,1,8,128]{4,1,3,2,0:T(8,128)(2,1)S(1)}, bf16[1,32,1,8,128]{4,1,3,2,0:T(8,128)(2,1)S(1)}, u32[]{:S(2)}, u32[]{:S(2)}) collective-permute-start(bf16[1,32,1,8,128]{4,1,3,2,0:T(8,128)(2,1)S(1)} %get-tuple-element.110), channel_id=1, source_target_pairs={{0,2},{2,4},{4,6},{6,8},{8,10},{10,12},{12,14},{14,0},{1,3},{3,5},... | collective-permute-start | bytes 196616 | tf_op jit(solution)/shard_map/ppermute | solution.py:14
  20.3 2.7 copy-start.1
  23.1 11.4 %collective-permute-start.10 = (bf16[1,32,7,8,1]{4,1,3,2,0:T(8,128)(2,1)S(1)}, bf16[1,32,7,8,1]{4,1,3,2,0:T(8,128)(2,1)S(1)}, u32[]{:S(2)}, u32[]{:S(2)}) collective-permute-start(bf16[1,32,7,8,1]{4,1,3,2,0:T(8,128)(2,1)S(1)} %get-tuple-element.89), channel_id=1, source_target_pairs={{0,1},{1,0},{2,3},{3,2},{4,5},{5,4},{6,7},{7,6},{8,9},{9,8},{10,11... | collective-permute-start | bytes 10760 | tf_op jit(solution)/shard_map/ppermute | solution.py:14
  26.5 17.9 %collective-permute-start.11 = (bf16[1,32,7,8,1]{4,1,3,2,0:T(8,128)(2,1)S(1)}, bf16[1,32,7,8,1]{4,1,3,2,0:T(8,128)(2,1)S(1)}, u32[]{:S(2)}, u32[]{:S(2)}) collective-permute-start(bf16[1,32,7,8,1]{4,1,3,2,0:T(8,128)(2,1)S(1)} %get-tuple-element.90), channel_id=1, source_target_pairs={{1,0},{0,1},{3,2},{2,3},{5,4},{4,5},{7,6},{6,7},{9,8},{8,9},{11,10... | collective-permute-start | bytes 10760 | tf_op jit(solution)/shard_map/ppermute | solution.py:15
  26.8 27.4 %collective-permute-start.2 = (bf16[1,32,7,8,1]{4,1,3,2,0:T(8,128)(2,1)S(1)}, bf16[1,32,7,8,1]{4,1,3,2,0:T(8,128)(2,1)S(1)}, u32[]{:S(2)}, u32[]{:S(2)}) collective-permute-start(bf16[1,32,7,8,1]{4,1,3,2,0:T(8,128)(2,1)S(1)} %get-tuple-element.97), channel_id=1, source_target_pairs={{0,1},{1,0},{2,3},{3,2},{4,5},{5,4},{6,7},{7,6},{8,9},{9,8},{10,11... | collective-permute-start | bytes 10760 | tf_op jit(solution)/shard_map/ppermute | solution.py:14
  29.8 34.3 %collective-permute-start.3 = (bf16[1,32,7,8,1]{4,1,3,2,0:T(8,128)(2,1)S(1)}, bf16[1,32,7,8,1]{4,1,3,2,0:T(8,128)(2,1)S(1)}, u32[]{:S(2)}, u32[]{:S(2)}) collective-permute-start(bf16[1,32,7,8,1]{4,1,3,2,0:T(8,128)(2,1)S(1)} %get-tuple-element.98), channel_id=1, source_target_pairs={{1,0},{0,1},{3,2},{2,3},{5,4},{4,5},{7,6},{6,7},{9,8},{8,9},{11,10... | collective-permute-start | bytes 10760 | tf_op jit(solution)/shard_map/ppermute | solution.py:15
  70.4 0.7 copy-start.5
  82.3 5.3 %collective-permute-start.4 = (bf16[1,32,1,8,128]{4,1,3,2,0:T(8,128)(2,1)S(1)}, bf16[1,32,1,8,128]{4,1,3,2,0:T(8,128)(2,1)S(1)}, u32[]{:S(2)}, u32[]{:S(2)}) collective-permute-start(bf16[1,32,1,8,128]{4,1,3,2,0:T(8,128)(2,1)S(1)} %get-tuple-element.107), channel_id=1, source_target_pairs={{0,2},{2,4},{4,6},{6,8},{8,10},{10,12},{12,14},{14,0},{1,3},{3,5},... | collective-permute-start | bytes 196616 | tf_op jit(solution)/shard_map/ppermute | solution.py:14
  82.4 5.2 %collective-permute-start.5 = (bf16[1,32,1,8,128]{4,1,3,2,0:T(8,128)(2,1)S(1)}, bf16[1,32,1,8,128]{4,1,3,2,0:T(8,128)(2,1)S(1)}, u32[]{:S(2)}, u32[]{:S(2)}) collective-permute-start(bf16[1,32,1,8,128]{4,1,3,2,0:T(8,128)(2,1)S(1)} %get-tuple-element.108), channel_id=1, source_target_pairs={{2,0},{4,2},{6,4},{8,6},{10,8},{12,10},{14,12},{0,14},{3,1},{5,3},... | collective-permute-start | bytes 196616 | tf_op jit(solution)/shard_map/ppermute | solution.py:15
  87.9 82.2 %collective-permute-start.6 = (bf16[1,32,7,8,1]{4,1,3,2,0:T(8,128)(2,1)S(1)}, bf16[1,32,7,8,1]{4,1,3,2,0:T(8,128)(2,1)S(1)}, u32[]{:S(2)}, u32[]{:S(2)}) collective-permute-start(bf16[1,32,7,8,1]{4,1,3,2,0:T(8,128)(2,1)S(1)} %get-tuple-element.93), channel_id=1, source_target_pairs={{0,1},{1,0},{2,3},{3,2},{4,5},{5,4},{6,7},{7,6},{8,9},{9,8},{10,11... | collective-permute-start | bytes 10760 | tf_op jit(solution)/shard_map/ppermute | solution.py:14
  90.7 79.5 %collective-permute-start.7 = (bf16[1,32,7,8,1]{4,1,3,2,0:T(8,128)(2,1)S(1)}, bf16[1,32,7,8,1]{4,1,3,2,0:T(8,128)(2,1)S(1)}, u32[]{:S(2)}, u32[]{:S(2)}) collective-permute-start(bf16[1,32,7,8,1]{4,1,3,2,0:T(8,128)(2,1)S(1)} %get-tuple-element.94), channel_id=1, source_target_pairs={{1,0},{0,1},{3,2},{2,3},{5,4},{4,5},{7,6},{6,7},{9,8},{8,9},{11,10... | collective-permute-start | bytes 10760 | tf_op jit(solution)/shard_map/ppermute | solution.py:15
  182.9 0.9 copy-start.6
  327.2 1.9 copy-start.3
Sparse Core Ops, SparseCore 0:
  184.0 143.2 all-reduce.6
where the time goes:
time: 337 us
  waiting for transfers between devices  178 us (53%)
  blocking collectives  78.4 us (23%)
  starting transfers between devices  21.6 us (6%)
  matrix products  21.5 us (6%)
  between operations  14.6 us (4%)
  local copies, waits for them, and re-layouts  14 us (4%)
  other arithmetic  8.32 us (2%)
    psum x1, waiting for transfers between devices, shards(): lax.psum((first_grad, first_bgrad, second_grad, second_bgrad), ('smp', 'g...  142 us
    psum x1, blocking collectives, shards(): lax.psum((first_grad, first_bgrad, second_grad, second_bgrad), ('smp', 'g...  78.4 us
    ppermute x6, waiting for transfers between devices, extended(): after = lax.ppermute(initial, axis, down)  19.7 us
    ppermute x6, waiting for transfers between devices, extended(): before = lax.ppermute(last, axis, up)  16.3 us
    dot_general x18, matrix products, correlate(): jnp.einsum('soxyz,skxyz->ok', upstream, stacked, preferred_element_type=j...  12.8 us
    ppermute x6, starting transfers between devices, extended(): after = lax.ppermute(initial, axis, down)  12.4 us
    ppermute x6, starting transfers between devices, extended(): before = lax.ppermute(last, axis, up)  9.18 us
    dot_general x27, matrix products, convolve(): jnp.einsum('ok,skxyz->soxyz', tap_block, stacked, preferred_element_type=...  8.76 us
  transfers between devices with their start and end apart: 13, of which 7 were waited for; matrix products, arithmetic and copies ran while one was open for 2% of the time, Pallas kernels for 0%

commit v1 on v0

v1 whole, which is shorter than its diff:
```python
import functools

import jax
import jax.numpy as jnp
from jax import lax
from jax.experimental import pallas as pl
from jax.experimental.pallas import tpu as pltpu
from jax.sharding import PartitionSpec as P

MESH = pl.DeviceIdType.MESH
BF = jnp.bfloat16
F32 = jnp.float32
LANES = 128
PAY = 640


def kernel(sizes, scale, ft, ct, w1, w2, w2t, b1, b2, out, g1, gb1, g2, gb2,
           sf, sc, sh, eo, ei, wa, wb, wv, dd, pg, pay, snd, ra, mid, rb, fin, rc,
           hs, hr, as_, ar, bs, br, cs, cr):
    ns, nx, nz = sizes
    ng = nx * nz
    rows = PAY // ng
    smp, gx, gz = lax.axis_index("smp"), lax.axis_index("gx"), lax.axis_index("gz")
    me = gx * nz + gz
    left, right = lax.rem(gx + nx - 1, nx), lax.rem(gx + 1, nx)
    other = 1 - gz
    lane = lax.broadcasted_iota(jnp.int32, (32, LANES), 1)
    half = lane // 2

    def in_group(d):
        peer = lax.rem(me + d, ng)
        return peer, (smp, peer // nz, lax.rem(peer, nz))

    def in_samples(d):
        peer = lax.rem(smp + d, ns)
        return peer, (peer, gx, gz)

    barrier = pltpu.get_barrier_semaphore()

    @pl.loop(1, ng)
    def _(d):
        pl.semaphore_signal(barrier, inc=1, device_id=in_group(d)[1], device_id_type=MESH)

    @pl.loop(1, ns)
    def _(d):
        pl.semaphore_signal(barrier, inc=1, device_id=in_samples(d)[1], device_id_type=MESH)

    def edges(s, f):
        def body(j, acc):
            row = pl.multiple_of(lax.rem(j, 8) * 32, 32)
            blk = s[1, 1 + j // 8, pl.ds(row, 32), :].astype(F32)
            return jnp.where(half == j, pltpu.roll(blk, 2 * j + 1, 1), acc)

        eo[f] = lax.fori_loop(0, 40, body, jnp.zeros((32, LANES), F32), unroll=8).astype(BF)

    def halo(s, f):
        plan = (
            (2, eo.at[f], ei.at[f, 1], (smp, gx, other)),
            (3, eo.at[f], ei.at[f, 2], (smp, left, other)),
            (4, eo.at[f], ei.at[f, 0], (smp, right, other)),
            (0, s.at[1, 1], s.at[1, 6], (smp, left, gz)),
            (1, s.at[1, 5], s.at[1, 0], (smp, right, gz)),
        )
        return [
            pltpu.make_async_remote_copy(
                src_ref=src, dst_ref=dst, send_sem=hs.at[f, i], recv_sem=hr.at[f, i],
                device_id=dev, device_id_type=MESH,
            )
            for i, src, dst, dev in plan
        ]

    def shift(s, f):
        for slots, which, first in (((1, 6), 1, 0), ((0, 1), 0, 32), ((6, 7), 2, 0)):
            edge = ei[f, which].astype(F32)

            def body(j, carry, edge=edge, first=first, slot0=slots[0]):
                slot = slot0 + j // 8
                row = pl.multiple_of(lax.rem(j, 8) * 32, 32)
                blk = s[1, slot, pl.ds(row, 32), :].astype(F32)
                e = pltpu.roll(edge, 127 - 2 * (first + j), 1)
                s[0, slot, pl.ds(row, 32), :] = pltpu.roll(jnp.where(lane == 127, e, blk), 1, 1).astype(BF)
                s[2, slot, pl.ds(row, 32), :] = pltpu.roll(jnp.where(lane == 0, e, blk), 127, 1).astype(BF)
                return carry

            lax.fori_loop(0, 8 * (slots[1] - slots[0]), body, 0, unroll=8)

    def banded(dst, tap):
        zero = jnp.zeros((32, LANES), F32)
        for k in range(9):
            a, c = k // 3, k % 3
            parts = [tap(a * 9 + b * 3 + c).astype(F32) for b in range(3)]
            base = jnp.concatenate(parts + [jnp.zeros((32, 32), F32)], axis=1)
            r = [pltpu.roll(base, (32 * (m + 3)) % LANES, 1) if m != 1 else base for m in range(4)]
            low, mid_, top = lane < 32, lane < 64, lane >= 96
            tiles = (
                (jnp.where(mid_, r[0], 0.0), zero),
                (r[1], zero),
                (r[2], zero),
                (jnp.where(mid_, 0.0, r[3]), jnp.where(low, r[3], 0.0)),
                (jnp.where(top, r[0], 0.0), jnp.where(mid_, r[0], 0.0)),
                (zero, r[1]),
                (zero, r[2]),
                (zero, jnp.where(mid_, 0.0, r[3])),
            )
            for y, pair in enumerate(tiles):
                for t in range(2):
                    dst[k, y * 32:(y + 1) * 32, t * LANES:(t + 1) * LANES] = pair[t].astype(BF)

    def conv(w, s, xs):
        lhs = jnp.concatenate([w[k] for k in range(9)], axis=1)
        rhs = jnp.concatenate(
            [jnp.concatenate([s[k % 3, x + k // 3] for x in xs], axis=1) for k in range(9)], axis=0)
        return jnp.dot(lhs, rhs, preferred_element_type=F32)

    def diagonal(g):
        t = [[g[y * 32:(y + 1) * 32, u * LANES:(u + 1) * LANES] for u in range(2)] for y in range(8)]
        x0 = jnp.where(lane < 64, t[0][0] + t[4][1], jnp.where(lane >= 96, t[4][0], 0.0))
        x1 = t[1][0] + t[5][1]
        x2 = t[2][0] + t[6][1]
        x3 = jnp.where(lane >= 64, t[3][0] + t[7][1], jnp.where(lane < 32, t[3][1], 0.0))
        total = pltpu.roll(x0, 32, 1) + x1 + pltpu.roll(x2, 96, 1) + pltpu.roll(x3, 64, 1)
        return jnp.where(lane < 96, total, 0.0)

    def column(ref):
        row = lax.broadcasted_iota(jnp.int32, (32, 32), 0)
        col = lax.broadcasted_iota(jnp.int32, (32, 32), 1)
        one = jnp.sum(jnp.where(row == col, jnp.broadcast_to(ref[...], (32, 32)), 0.0), axis=1, keepdims=True)
        return jnp.concatenate([one] * 8, axis=0)

    for x in range(5):
        sf[1, 1 + x] = ft[x]
        sc[1, 1 + x] = ct[x]
    edges(sf, 0)
    edges(sc, 1)
    pl.semaphore_wait(barrier, ng + ns - 2)
    moves_f = halo(sf, 0)
    for m in moves_f:
        m.start()
    moves_c = halo(sc, 1)
    for m in moves_c:
        m.start()

    banded(wa, lambda i: w1[i])
    banded(wv, lambda i: w2t[26 - i])
    banded(wb, lambda i: w2[i])

    for m in moves_f:
        m.wait_recv()
    shift(sf, 0)
    tiles = ((0, 1), (2, 3), (4,))
    bias = column(b1)
    for xs in tiles:
        v = conv(wa, sf, xs) + bias
        q = 1.0 / (1.0 + jnp.exp(-v))
        h = (v * q).astype(BF)
        d = q * (1.0 + v * (1.0 - q))
        for i, x in enumerate(xs):
            sh[1, 1 + x] = h[:, i * LANES:(i + 1) * LANES]
            dd[x] = d[:, i * LANES:(i + 1) * LANES]
    edges(sh, 2)
    moves_h = halo(sh, 2)
    for m in moves_h:
        m.start()

    for m in moves_c:
        m.wait_recv()
    shift(sc, 1)
    sums = jnp.zeros((256, LANES), F32)
    for xs in tiles:
        u = conv(wv, sc, xs)
        for i, x in enumerate(xs):
            p = (u[:, i * LANES:(i + 1) * LANES] * dd[x]).astype(BF)
            pg[x] = p
            sums = sums + p.astype(F32)

    def spans(s, c, a):
        return jnp.concatenate([s[c, a + x] for x in range(5)], axis=1)

    def nt(p, r):
        return lax.dot_general(p, r, (((1,), (1,)), ((), ())), preferred_element_type=F32)

    for k in range(9):
        a, c = k // 3, k % 3
        upstream = jnp.concatenate([pg[x] for x in range(5)], axis=1)
        pay[k * 32:(k + 1) * 32] = diagonal(nt(upstream, spans(sf, c, a)))
    for k in range(9):
        a, c = k // 3, k % 3
        own = jnp.concatenate([sh[1, 1 + x] for x in range(5)], axis=1)
        pay[288 + k * 32:288 + (k + 1) * 32] = diagonal(nt(spans(sc, 2 - c, 2 - a), own))

    def folded(v):
        total = v[0:32]
        for y in range(1, 8):
            total = total + v[y * 32:(y + 1) * 32]
        return jnp.sum(total, axis=1, keepdims=True)

    csum = jnp.zeros((256, LANES), F32)
    for x in range(5):
        csum = csum + ct[x].astype(F32)
    pay[576:608] = jnp.where(lane == 0, folded(sums), jnp.where(lane == 1, folded(csum), 0.0))
    pay[608:640] = jnp.zeros((32, LANES), F32)

    for s in range(ng):
        snd[s] = pay[s * rows:(s + 1) * rows].astype(BF)

    def send_a(d):
        peer, dev = in_group(d)
        return pltpu.make_async_remote_copy(
            src_ref=snd.at[peer], dst_ref=ra.at[me], send_sem=as_.at[peer], recv_sem=ar.at[me],
            device_id=dev, device_id_type=MESH)

    def from_a(d):
        peer, dev = in_group(d)
        return pltpu.make_async_remote_copy(
            src_ref=snd.at[peer], dst_ref=ra.at[peer], send_sem=as_.at[peer], recv_sem=ar.at[peer],
            device_id=dev, device_id_type=MESH)

    @pl.loop(1, ng)
    def _(d):
        send_a(d).start()

    ra[me] = snd[me]

    for m in moves_h:
        m.wait_recv()
    shift(sh, 2)
    bias2 = column(b2)
    for xs in tiles:
        v = conv(wb, sh, xs) + bias2
        for i, x in enumerate(xs):
            out[x] = (v[:, i * LANES:(i + 1) * LANES] + ft[x].astype(F32)).astype(BF)

    @pl.loop(1, ng)
    def _(d):
        from_a(d).wait_recv()

    def total(ref, n):
        acc = ref[0].astype(F32)
        for s in range(1, n):
            acc = acc + ref[s].astype(F32)
        return acc

    mid[...] = total(ra, ng).astype(BF)

    def send_b(d):
        peer, dev = in_samples(d)
        return pltpu.make_async_remote_copy(
            src_ref=mid, dst_ref=rb.at[smp], send_sem=bs.at[peer], recv_sem=br.at[smp],
            device_id=dev, device_id_type=MESH)

    def from_b(d):
        peer, dev = in_samples(d)
        return pltpu.make_async_remote_copy(
            src_ref=mid, dst_ref=rb.at[peer], send_sem=bs.at[peer], recv_sem=br.at[peer],
            device_id=dev, device_id_type=MESH)

    @pl.loop(1, ns)
    def _(d):
        send_b(d).start()

    rb[smp] = mid[...]

    @pl.loop(1, ns)
    def _(d):
        from_b(d).wait_recv()

    fin[...] = (total(rb, ns) * scale).astype(BF)

    def send_c(d):
        peer, dev = in_group(d)
        return pltpu.make_async_remote_copy(
            src_ref=fin, dst_ref=rc.at[me], send_sem=cs.at[peer], recv_sem=cr.at[me],
            device_id=dev, device_id_type=MESH)

    def from_c(d):
        peer, dev = in_group(d)
        return pltpu.make_async_remote_copy(
            src_ref=fin, dst_ref=rc.at[peer], send_sem=cs.at[peer], recv_sem=cr.at[peer],
            device_id=dev, device_id_type=MESH)

    @pl.loop(1, ng)
    def _(d):
        send_c(d).start()

    rc[me] = fin[...]

    @pl.loop(1, ng)
    def _(d):
        from_c(d).wait_recv()

    for s in range(ng):
        pay[s * rows:(s + 1) * rows] = rc[s].astype(F32)
    for base, ref in ((0, g1), (288, g2)):
        for k in range(9):
            a, c = k // 3, k % 3
            blk = pay[base + k * 32:base + (k + 1) * 32]
            for b in range(3):
                ref[a * 9 + b * 3 + c] = blk[:, b * 32:(b + 1) * 32]
    tail = pay[576:608]
    row = lax.broadcasted_iota(jnp.int32, (32, 32), 0)
    col = lax.broadcasted_iota(jnp.int32, (32, 32), 1)
    for i, ref in ((0, gb1), (1, gb2)):
        ref[...] = jnp.sum(jnp.where(row == col, tail[:, i:i + 1], 0.0), axis=0, keepdims=True)

    for m in moves_f + moves_c + moves_h:
        m.wait_send()

    @pl.loop(1, ng)
    def _(d):
        send_a(d).wait_send()

    @pl.loop(1, ns)
    def _(d):
        send_b(d).wait_send()

    @pl.loop(1, ng)
    def _(d):
        send_c(d).wait_send()


def solution(mesh):
    sizes = tuple(mesh.shape[n] for n in ("smp", "gx", "gz"))
    ns, nx, nz = sizes
    ng = nx * nz
    rows = PAY // ng

    def slabs(field):
        return field[0].transpose(1, 2, 0, 3).reshape(5, 256, LANES)

    def shards(features, first_weight, first_bias, second_weight, second_bias, cotangent):
        cells = ns * nx * nz * 5 * 8 * LANES
        w1 = first_weight.transpose(1, 2, 3, 0, 4).reshape(27, 32, 32)
        w2 = second_weight.transpose(1, 2, 3, 0, 4).reshape(27, 32, 32)
        w2t = second_weight.transpose(1, 2, 3, 4, 0).reshape(27, 32, 32)
        vm = pl.BlockSpec(memory_space=pltpu.VMEM)
        dma = pltpu.SemaphoreType.DMA
        out, g1, gb1, g2, gb2 = pl.pallas_call(
            functools.partial(kernel, sizes, cells ** -0.5),
            out_shape=(
                jax.ShapeDtypeStruct((5, 256, LANES), BF),
                jax.ShapeDtypeStruct((27, 32, 32), F32),
                jax.ShapeDtypeStruct((1, 32), F32),
                jax.ShapeDtypeStruct((27, 32, 32), F32),
                jax.ShapeDtypeStruct((1, 32), F32),
            ),
            in_specs=[vm] * 7,
            out_specs=(vm,) * 5,
            scratch_shapes=[
                pltpu.VMEM((3, 7, 256, LANES), BF),
                pltpu.VMEM((3, 7, 256, LANES), BF),
                pltpu.VMEM((3, 7, 256, LANES), BF),
                pltpu.VMEM((3, 32, LANES), BF),
                pltpu.VMEM((3, 3, 32, LANES), BF),
                pltpu.VMEM((9, 256, 256), BF),
                pltpu.VMEM((9, 256, 256), BF),
                pltpu.VMEM((9, 256, 256), BF),
                pltpu.VMEM((5, 256, LANES), F32),
                pltpu.VMEM((5, 256, LANES), BF),
                pltpu.VMEM((PAY, LANES), F32),
                pltpu.VMEM((ng, rows, LANES), BF),
                pltpu.VMEM((ng, rows, LANES), BF),
                pltpu.VMEM((rows, LANES), BF),
                pltpu.VMEM((ns, rows, LANES), BF),
                pltpu.VMEM((rows, LANES), BF),
                pltpu.VMEM((ng, rows, LANES), BF),
                dma((3, 5)), dma((3, 5)),
                dma((ng,)), dma((ng,)), dma((ns,)), dma((ns,)), dma((ng,)), dma((ng,)),
            ],
            compiler_params=pltpu.CompilerParams(
                collective_id=0, has_side_effects=True, vmem_limit_bytes=48 << 20),
        )(slabs(features), slabs(cotangent), w1, w2, w2t, first_bias.reshape(1, 32), second_bias.reshape(1, 32))
        back = lambda g: g.reshape(3, 3, 3, 32, 32).transpose(3, 0, 1, 2, 4)
        output = out.reshape(5, 8, 32, LANES).transpose(2, 0, 1, 3)[None]
        return output, back(g1), gb1.reshape(32), back(g2), gb2.reshape(32)

    block = P("smp", None, "gx", None, "gz")
    return jax.shard_map(
        shards, mesh=mesh, in_specs=(block, P(), P(), P(), P(), block),
        out_specs=(block, P(), P(), P(), P()), check_vma=False)
```

time: 337 us -> 49.4 us (0.15)
  waiting for transfers between devices: 178 us -> 0 us
  blocking collectives: 78.4 us -> 0 us
  Pallas kernels: 0 us -> 42 us
  starting transfers between devices: 21.6 us -> 0 us
  matrix products: 21.5 us -> 0 us
  between operations: 14.6 us -> 0.7 us
  other arithmetic: 8.32 us -> 0 us
  local copies, waits for them, and re-layouts: 14 us -> 6.52 us
    psum x1 -> x0, waiting for transfers between devices: 142 us -> none  [shards(): lax.psum((first_grad, first_bgrad, second_grad, second_bgrad), ('smp', 'g...]
    psum x1 -> x0, blocking collectives: 78.4 us -> none  [shards(): lax.psum((first_grad, first_bgrad, second_grad, second_bgrad), ('smp', 'g...]
    pallas_call x0 -> x1, Pallas kernels: none -> 42 us  [shards(): pl.pallas_call(functools.partial(kernel, sizes, cells ** (-0.5)), out_sha...]
    ppermute x12 -> x0, waiting for transfers between devices: 36 us -> none  [the longest x6 19.7 us: extended(): after = lax.ppermute(initial, axis, down)]
    ppermute x12 -> x0, starting transfers between devices: 21.5 us -> none  [the longest x6 12.4 us: extended(): after = lax.ppermute(initial, axis, down)]
    dot_general x45 -> x0, matrix products: 21.5 us -> none  [the longest x18 12.8 us: correlate(): jnp.einsum('soxyz,skxyz->ok', upstream, stacked, preferred_element_type=j...]
    concatenate x15 -> x0, other arithmetic: 6.25 us -> none  [the longest x7 3.72 us: extended(): array = jnp.concatenate([before, array, after], axis=dim)]
    slice x31 -> x0, local copies, waits for them, and re-layouts: 6.08 us -> none  [the longest x4 5.01 us: stack_taps(): padded[:, :, offset_x:offset_x + cells_x, offset_y:offset_y + cells_y, of...]
  transfers between devices with their start and end apart: 13 -> 0, of which waited for: 7 -> 0; matrix products, arithmetic and copies ran while one was open for 2% -> 0% of each run, Pallas kernels for 0% -> 0%
where the time goes in v1:
time: 49.4 us; the launch traced here: 49.2 us
  Pallas kernels  42 us (85%)
  local copies, waits for them, and re-layouts  6.52 us (13%)
  between operations  0.7 us (1%)
    pallas_call x1, Pallas kernels, shards(): pl.pallas_call(functools.partial(kernel, sizes, cells ** (-0.5)), out_sha...  42 us
    unnamed x16, local copies, waits for them, and re-layouts  4.43 us
    transpose x1, local copies, waits for them, and re-layouts, shards(): w2t = second_weight.transpose(1, 2, 3, 4, 0).reshape(27, 32, 32)  1.13 us

profile of v1, /device:TPU:1, one launch (start us, length us, event | category | flops | bytes accessed | tf_op | source)
XLA Modules:
  0.0 49.2 jit_solution(14132408102967445145)
XLA Ops:
  0.6 0.0 copy-start.4
  0.6 1.1 %copy.13 = bf16[3,3,3,32,32]{4,3,2,1,0:T(8,128)(2,1)S(1)} copy(bf16[3,3,3,32,32]{3,4,2,1,0:T(8,128)(2,1)} %bitcast.34) | data formatting | bytes 110592 | tf_op jit(solution)/shard_map/transpose | solution.py:334
  1.8 0.0 copy-done.4
  1.8 0.0 copy-start.5
  1.8 0.1 copy.11
  1.9 0.9 %copy-done.5 = bf16[1,32,5,8,128]{4,3,2,1,0:T(8,128)(2,1)S(1)} copy-done((bf16[1,32,5,8,128]{4,3,2,1,0:T(8,128)(2,1)S(1)}, bf16[1,32,5,8,128]{4,3,2,1,0:T(8,128)(2,1)}, u32[]{:S(2)}) %copy-start.5) | copy-done | bytes 327704
  2.8 0.0 copy-start
  2.8 0.0 copy-start.1
  2.8 0.1 copy.12
  2.8 0.0 copy-start.2
  2.8 0.0 copy-start.3
  2.9 0.8 %copy-done = bf16[32,3,3,3,32]{4,0,3,2,1:T(8,128)(2,1)S(1)} copy-done((bf16[32,3,3,3,32]{4,0,3,2,1:T(8,128)(2,1)S(1)}, bf16[32,3,3,3,32]{4,0,3,2,1:T(8,128)(2,1)}, u32[]{:S(2)}) %copy-start) | copy-done | bytes 55320
  3.7 0.1 copy-done.1
  3.8 0.0 copy-done.2
  3.8 0.0 copy-done.3
  3.8 42.0 %shard_map.101 = (bf16[5,256,128]{2,1,0:T(8,128)(2,1)S(1)}, f32[27,32,32]{2,1,0:T(8,128)S(1)}, f32[1,32]{1,0:T(1,128)S(1)}, f32[27,32,32]{2,1,0:T(8,128)S(1)}, f32[1,32]{1,0:T(1,128)S(1)}) custom-call(bf16[5,256,128]{2,1,0:T(8,128)(2,1)S(1)} %bitcast.32, bf16[5,256,128]{2,1,0:T(8,128)(2,1)S(1)} %bitcast.33, bf16[27,32,32]{2,1,0:T(8,128)(2,1)S(1)} %bitcast.40, ...), custom_call_target="tpu_custom_call" | custom-call | tf_op jit(solution)/shard_map/pallas_call | solution.py:337
  45.8 0.9 %copy.16 = bf16[5,8,32,128]{3,1,0,2:T(8,128)(2,1)} copy(bf16[5,8,32,128]{3,2,1,0:T(8,128)(2,1)S(1)} %bitcast.39) | data formatting | bytes 655360 | tf_op jit(solution)/shard_map/reshape | solution.py:373
  46.7 0.8 %copy.21 = f32[32,3,3,3,32]{4,0,3,2,1:T(8,128)} copy(f32[32,3,3,3,32]{4,0,3,2,1:T(8,128)S(1)} %bitcast.38) | data formatting | bytes 221184
  47.5 0.5 %copy.22 = f32[32]{0:T(128)} copy(f32[32]{0:T(128)S(1)} %bitcast.44) | data formatting | bytes 256
  48.0 0.8 %copy.23 = f32[32,3,3,3,32]{4,0,3,2,1:T(8,128)} copy(f32[32,3,3,3,32]{4,0,3,2,1:T(8,128)S(1)} %bitcast.37) | data formatting | bytes 221184
  48.7 0.5 %copy.24 = f32[32]{0:T(128)} copy(f32[32]{0:T(128)S(1)} %bitcast.43) | data formatting | bytes 256
Async XLA Ops:
  0.6 1.1 %copy-start.4 = (bf16[1,32,5,8,128]{4,3,2,1,0:T(8,128)(2,1)S(1)}, bf16[1,32,5,8,128]{4,3,2,1,0:T(8,128)(2,1)}, u32[]{:S(2)}) copy-start(bf16[1,32,5,8,128]{4,3,2,1,0:T(8,128)(2,1)} %param.6) | copy-start | bytes 983044
  1.8 1.0 %copy-start.5 = (bf16[1,32,5,8,128]{4,3,2,1,0:T(8,128)(2,1)S(1)}, bf16[1,32,5,8,128]{4,3,2,1,0:T(8,128)(2,1)}, u32[]{:S(2)}) copy-start(bf16[1,32,5,8,128]{4,3,2,1,0:T(8,128)(2,1)} %param.11) | copy-start | bytes 983044
  2.8 0.9 %copy-start = (bf16[32,3,3,3,32]{4,0,3,2,1:T(8,128)(2,1)S(1)}, bf16[32,3,3,3,32]{4,0,3,2,1:T(8,128)(2,1)}, u32[]{:S(2)}) copy-start(bf16[32,3,3,3,32]{4,0,3,2,1:T(8,128)(2,1)} %param.9) | copy-start | bytes 165892
  2.8 1.0 %copy-start.1 = (bf16[32,3,3,3,32]{4,0,3,2,1:T(8,128)(2,1)S(1)}, bf16[32,3,3,3,32]{4,0,3,2,1:T(8,128)(2,1)}, u32[]{:S(2)}) copy-start(bf16[32,3,3,3,32]{4,0,3,2,1:T(8,128)(2,1)} %param.7) | copy-start | bytes 165892
  2.8 1.0 %copy-start.2 = (f32[32]{0:T(128)S(1)}, f32[32]{0:T(128)}, u32[]{:S(2)}) copy-start(f32[32]{0:T(128)} %param.8) | copy-start | bytes 388
  2.8 1.0 %copy-start.3 = (f32[32]{0:T(128)S(1)}, f32[32]{0:T(128)}, u32[]{:S(2)}) copy-start(f32[32]{0:T(128)} %param.10) | copy-start | bytes 388

commit v2 on v1

--- a/solution.py
+++ b/solution.py
@@ -14,9 +14,10 @@
 PAY = 640
 
 
-def kernel(sizes, scale, ft, ct, w1, w2, w2t, b1, b2, out, g1, gb1, g2, gb2,
-           sf, sc, sh, eo, ei, wa, wb, wv, dd, pg, pay, snd, ra, mid, rb, fin, rc,
-           hs, hr, as_, ar, bs, br, cs, cr):
+def kernel(sizes, scale, feat, cot, w1h, w2h, b1h, b2h, rc, out,
+           vf, vc, w1, w2, b1, b2, pm, pe, ps,
+           sf, sc, sh, eo, ei, wa, wb, wv, dd, pg, pay, snd, ra, mid, rb, fin,
+           ins, hs, hr, as_, ar, bs, br, cs, cr):
     ns, nx, nz = sizes
     ng = nx * nz
     rows = PAY // ng
@@ -25,7 +26,7 @@
     left, right = lax.rem(gx + nx - 1, nx), lax.rem(gx + 1, nx)
     other = 1 - gz
     lane = lax.broadcasted_iota(jnp.int32, (32, LANES), 1)
-    half = lane // 2
+    level = lax.rem(lane // 2, 8)
 
     def in_group(d):
         peer = lax.rem(me + d, ng)
@@ -35,6 +36,15 @@
         peer = lax.rem(smp + d, ns)
         return peer, (peer, gx, gz)
 
+    load_f = [pltpu.make_async_copy(feat.at[:, x], vf.at[x], ins.at[x]) for x in range(5)]
+    load_c = [pltpu.make_async_copy(cot.at[:, x], vc.at[x], ins.at[5 + x]) for x in range(5)]
+    load_w = [
+        pltpu.make_async_copy(src, dst, ins.at[10 + i])
+        for i, (src, dst) in enumerate(((w1h, w1), (w2h, w2), (b1h, b1), (b2h, b2)))
+    ]
+    for m in load_f + load_c + load_w:
+        m.start()
+
     barrier = pltpu.get_barrier_semaphore()
 
     @pl.loop(1, ng)
@@ -45,13 +55,42 @@
     def _(d):
         pl.semaphore_signal(barrier, inc=1, device_id=in_samples(d)[1], device_id_type=MESH)
 
+    def grid(height, width):
+        return (lax.broadcasted_iota(jnp.int32, (height, width), 0),
+                lax.broadcasted_iota(jnp.int32, (height, width), 1))
+
+    def hot(cond):
+        return jnp.where(cond, 1.0, 0.0).astype(BF)
+
+    def constants():
+        r, c = grid(256, 256)
+        pm[...] = hot((r // 32 == lax.rem(c, 8)) & (lax.rem(r, 32) == c // 8))
+        r, c = grid(LANES, LANES)
+        side = lax.rem(c, 2)
+        for x in range(5):
+            pe[x * LANES:(x + 1) * LANES] = hot(
+                (c // 16 == x) & (((r == LANES - 1) & (side == 0)) | ((r == 0) & (side == 1))))
+        r, c = grid(LANES, 256)
+        near = hot(((c < LANES) & (c == r + 1)) | ((c >= LANES) & (c == r + LANES - 1)))
+        r2 = lax.rem(r, 2)
+        ends = ((r2 == 0) & (c == 0)) | ((r2 == 1) & (c == 255))
+        for x in range(5):
+            ps[x, 0:LANES] = near
+            ps[x, LANES:256] = hot((r // 16 == x) & ends)
+
+    def rows_in(s, v):
+        slab = jnp.concatenate([v[x].reshape(256, LANES) for x in range(5)], axis=1)
+        moved = jnp.dot(pm[...], slab, preferred_element_type=F32).astype(BF)
+        for x in range(5):
+            s[1, 1 + x] = moved[:, x * LANES:(x + 1) * LANES]
+
     def edges(s, f):
-        def body(j, acc):
-            row = pl.multiple_of(lax.rem(j, 8) * 32, 32)
-            blk = s[1, 1 + j // 8, pl.ds(row, 32), :].astype(F32)
-            return jnp.where(half == j, pltpu.roll(blk, 2 * j + 1, 1), acc)
-
-        eo[f] = lax.fori_loop(0, 40, body, jnp.zeros((32, LANES), F32), unroll=8).astype(BF)
+        slab = jnp.concatenate([s[1, 1 + x] for x in range(5)], axis=1)
+        picked = jnp.dot(slab, pe[...], preferred_element_type=F32)
+        acc = jnp.zeros((32, LANES), F32)
+        for y in range(8):
+            acc = jnp.where(level == y, picked[y * 32:(y + 1) * 32], acc)
+        eo[f] = jnp.where(lane < 80, acc, 0.0).astype(BF)
 
     def halo(s, f):
         plan = (
@@ -70,26 +109,22 @@
         ]
 
     def shift(s, f):
-        for slots, which, first in (((1, 6), 1, 0), ((0, 1), 0, 32), ((6, 7), 2, 0)):
-            edge = ei[f, which].astype(F32)
-
-            def body(j, carry, edge=edge, first=first, slot0=slots[0]):
-                slot = slot0 + j // 8
-                row = pl.multiple_of(lax.rem(j, 8) * 32, 32)
-                blk = s[1, slot, pl.ds(row, 32), :].astype(F32)
-                e = pltpu.roll(edge, 127 - 2 * (first + j), 1)
-                s[0, slot, pl.ds(row, 32), :] = pltpu.roll(jnp.where(lane == 127, e, blk), 1, 1).astype(BF)
-                s[2, slot, pl.ds(row, 32), :] = pltpu.roll(jnp.where(lane == 0, e, blk), 127, 1).astype(BF)
-                return carry
-
-            lax.fori_loop(0, 8 * (slots[1] - slots[0]), body, 0, unroll=8)
+        spread = []
+        for i in range(3):
+            e = ei[f, i].astype(F32)
+            spread.append(jnp.concatenate([jnp.where(level == y, e, 0.0) for y in range(8)], axis=0).astype(BF))
+        for slot in (1, 2, 3, 4, 5, 0, 6):
+            which, x = (0, 4) if slot == 0 else (2, 0) if slot == 6 else (1, slot - 1)
+            wide = jnp.concatenate([s[1, slot], spread[which]], axis=1)
+            moved = jnp.dot(wide, ps[x], preferred_element_type=F32).astype(BF)
+            s[0, slot] = moved[:, :LANES]
+            s[2, slot] = moved[:, LANES:]
 
     def banded(dst, tap):
         zero = jnp.zeros((32, LANES), F32)
         for k in range(9):
             a, c = k // 3, k % 3
-            parts = [tap(a * 9 + b * 3 + c).astype(F32) for b in range(3)]
-            base = jnp.concatenate(parts + [jnp.zeros((32, 32), F32)], axis=1)
+            base = jnp.concatenate(tap(a, c) + [jnp.zeros((32, 32), F32)], axis=1)
             r = [pltpu.roll(base, (32 * (m + 3)) % LANES, 1) if m != 1 else base for m in range(4)]
             low, mid_, top = lane < 32, lane < 64, lane >= 96
             tiles = (
@@ -127,22 +162,57 @@
         one = jnp.sum(jnp.where(row == col, jnp.broadcast_to(ref[...], (32, 32)), 0.0), axis=1, keepdims=True)
         return jnp.concatenate([one] * 8, axis=0)
 
-    for x in range(5):
-        sf[1, 1 + x] = ft[x]
-        sc[1, 1 + x] = ct[x]
+    def taps(w):
+        return lambda a, c: [w[a * 9 + b * 3 + c].astype(F32) for b in range(3)]
+
+    def turned(w):
+        def tap(a, c):
+            wide = jnp.concatenate([w[(2 - a) * 9 + (2 - b) * 3 + 2 - c].astype(F32) for b in range(3)]
+                                   + [jnp.zeros((32, 32), F32)], axis=1)
+            tall = wide.T
+            return [tall[b * 32:(b + 1) * 32] for b in range(3)]
+        return tap
+
+    constants()
+    for m in load_f:
+        m.wait()
+    rows_in(sf, vf)
     edges(sf, 0)
-    edges(sc, 1)
     pl.semaphore_wait(barrier, ng + ns - 2)
     moves_f = halo(sf, 0)
     for m in moves_f:
         m.start()
+    for m in load_c:
+        m.wait()
+    rows_in(sc, vc)
+    edges(sc, 1)
     moves_c = halo(sc, 1)
     for m in moves_c:
         m.start()
-
-    banded(wa, lambda i: w1[i])
-    banded(wv, lambda i: w2t[26 - i])
-    banded(wb, lambda i: w2[i])
+    for m in load_w:
+        m.wait()
+
+    banded(wa, taps(w1))
+    banded(wv, turned(w2))
+    banded(wb, taps(w2))
+
+    def folded(v):
+        total = v[0:32]
+        for y in range(1, 8):
+            total = total + v[y * 32:(y + 1) * 32]
+        return jnp.sum(total, axis=1, keepdims=True)
+
+    csum = jnp.zeros((256, LANES), F32)
+    for x in range(5):
+        csum = csum + sc[1, 1 + x].astype(F32)
+    csum = folded(csum)
+
+    def split(v, which):
+        both = v + pltpu.roll(v, LANES - 2, 1)
+        high = both.astype(BF).astype(F32)
+        lanes = lax.broadcasted_iota(jnp.int32, v.shape, 1)
+        pair = jnp.where(lanes < 2, high, pltpu.roll(both - high, 2, 1))
+        return jnp.where(which & (lanes < 4), pair, v).astype(BF)
 
     for m in moves_f:
         m.wait_recv()
@@ -188,20 +258,19 @@
         own = jnp.concatenate([sh[1, 1 + x] for x in range(5)], axis=1)
         pay[288 + k * 32:288 + (k + 1) * 32] = diagonal(nt(spans(sc, 2 - c, 2 - a), own))
 
-    def folded(v):
-        total = v[0:32]
-        for y in range(1, 8):
-            total = total + v[y * 32:(y + 1) * 32]
-        return jnp.sum(total, axis=1, keepdims=True)
-
-    csum = jnp.zeros((256, LANES), F32)
-    for x in range(5):
-        csum = csum + ct[x].astype(F32)
-    pay[576:608] = jnp.where(lane == 0, folded(sums), jnp.where(lane == 1, folded(csum), 0.0))
+    pay[576:608] = jnp.where(lane == 0, folded(sums), jnp.where(lane == 1, csum, 0.0))
     pay[608:640] = jnp.zeros((32, LANES), F32)
 
+    def bias_rows(first):
+        r = lax.broadcasted_iota(jnp.int32, (rows, LANES), 0) + first
+        return (r >= 576) & (r < 608)
+
     for s in range(ng):
-        snd[s] = pay[s * rows:(s + 1) * rows].astype(BF)
+        part = pay[s * rows:(s + 1) * rows]
+        if (s + 1) * rows > 576 and s * rows < 608:
+            snd[s] = split(part, bias_rows(s * rows))
+        else:
+            snd[s] = part.astype(BF)
 
     def send_a(d):
         peer, dev = in_group(d)
@@ -228,7 +297,9 @@
     for xs in tiles:
         v = conv(wb, sh, xs) + bias2
         for i, x in enumerate(xs):
-            out[x] = (v[:, i * LANES:(i + 1) * LANES] + ft[x].astype(F32)).astype(BF)
+            r = (v[:, i * LANES:(i + 1) * LANES] + sf[1, 1 + x].astype(F32)).astype(BF)
+            back = lax.dot_general(pm[...], r, (((0,), (0,)), ((), ())), preferred_element_type=F32)
+            out[x] = back.astype(BF)
 
     @pl.loop(1, ng)
     def _(d):
@@ -240,7 +311,8 @@
             acc = acc + ref[s].astype(F32)
         return acc
 
-    mid[...] = total(ra, ng).astype(BF)
+    mine = bias_rows(me * rows)
+    mid[...] = split(total(ra, ng), mine)
 
     def send_b(d):
         peer, dev = in_samples(d)
@@ -264,7 +336,7 @@
     def _(d):
         from_b(d).wait_recv()
 
-    fin[...] = (total(rb, ns) * scale).astype(BF)
+    fin[...] = split(total(rb, ns) * scale, mine)
 
     def send_c(d):
         peer, dev = in_group(d)
@@ -288,7 +360,27 @@
     def _(d):
         from_c(d).wait_recv()
 
-    for s in range(ng):
+    for m in moves_f + moves_c + moves_h:
+        m.wait_send()
+
+    @pl.loop(1, ng)
+    def _(d):
+        send_a(d).wait_send()
+
+    @pl.loop(1, ns)
+    def _(d):
+        send_b(d).wait_send()
+
+    @pl.loop(1, ng)
+    def _(d):
+        send_c(d).wait_send()
+
+
+def unpack(rows, rc, mid, out, g1, gb1, g2, gb2, pay, sem):
+    moves = [pltpu.make_async_copy(mid.at[x], out.at[:, x], sem.at[x]) for x in range(5)]
+    for m in moves:
+        m.start()
+    for s in range(PAY // rows):
         pay[s * rows:(s + 1) * rows] = rc[s].astype(F32)
     for base, ref in ((0, g1), (288, g2)):
         for k in range(9):
@@ -297,25 +389,13 @@
             for b in range(3):
                 ref[a * 9 + b * 3 + c] = blk[:, b * 32:(b + 1) * 32]
     tail = pay[576:608]
+    tail = tail + pltpu.roll(tail, LANES - 2, 1)
     row = lax.broadcasted_iota(jnp.int32, (32, 32), 0)
     col = lax.broadcasted_iota(jnp.int32, (32, 32), 1)
     for i, ref in ((0, gb1), (1, gb2)):
         ref[...] = jnp.sum(jnp.where(row == col, tail[:, i:i + 1], 0.0), axis=0, keepdims=True)
-
-    for m in moves_f + moves_c + moves_h:
-        m.wait_send()
-
-    @pl.loop(1, ng)
-    def _(d):
-        send_a(d).wait_send()
-
-    @pl.loop(1, ns)
-    def _(d):
-        send_b(d).wait_send()
-
-    @pl.loop(1, ng)
-    def _(d):
-        send_c(d).wait_send()
+    for m in moves:
+        m.wait()
 
 
 def solution(mesh):
@@ -324,28 +404,31 @@
     ng = nx * nz
     rows = PAY // ng
 
-    def slabs(field):
-        return field[0].transpose(1, 2, 0, 3).reshape(5, 256, LANES)
-
     def shards(features, first_weight, first_bias, second_weight, second_bias, cotangent):
         cells = ns * nx * nz * 5 * 8 * LANES
         w1 = first_weight.transpose(1, 2, 3, 0, 4).reshape(27, 32, 32)
         w2 = second_weight.transpose(1, 2, 3, 0, 4).reshape(27, 32, 32)
-        w2t = second_weight.transpose(1, 2, 3, 4, 0).reshape(27, 32, 32)
         vm = pl.BlockSpec(memory_space=pltpu.VMEM)
+        hbm = pl.BlockSpec(memory_space=pltpu.MemorySpace.HBM)
         dma = pltpu.SemaphoreType.DMA
-        out, g1, gb1, g2, gb2 = pl.pallas_call(
+        gathered, mid = pl.pallas_call(
             functools.partial(kernel, sizes, cells ** -0.5),
             out_shape=(
+                jax.ShapeDtypeStruct((ng, rows, LANES), BF),
                 jax.ShapeDtypeStruct((5, 256, LANES), BF),
-                jax.ShapeDtypeStruct((27, 32, 32), F32),
-                jax.ShapeDtypeStruct((1, 32), F32),
-                jax.ShapeDtypeStruct((27, 32, 32), F32),
-                jax.ShapeDtypeStruct((1, 32), F32),
             ),
-            in_specs=[vm] * 7,
-            out_specs=(vm,) * 5,
+            in_specs=[hbm] * 6,
+            out_specs=(vm,) * 2,
             scratch_shapes=[
+                pltpu.VMEM((5, 32, 8, LANES), BF),
+                pltpu.VMEM((5, 32, 8, LANES), BF),
+                pltpu.VMEM((27, 32, 32), BF),
+                pltpu.VMEM((27, 32, 32), BF),
+                pltpu.VMEM((1, 32), F32),
+                pltpu.VMEM((1, 32), F32),
+                pltpu.VMEM((256, 256), BF),
+                pltpu.VMEM((640, LANES), BF),
+                pltpu.VMEM((5, 256, 256), BF),
                 pltpu.VMEM((3, 7, 256, LANES), BF),
                 pltpu.VMEM((3, 7, 256, LANES), BF),
                 pltpu.VMEM((3, 7, 256, LANES), BF),
@@ -362,16 +445,29 @@
                 pltpu.VMEM((rows, LANES), BF),
                 pltpu.VMEM((ns, rows, LANES), BF),
                 pltpu.VMEM((rows, LANES), BF),
-                pltpu.VMEM((ng, rows, LANES), BF),
-                dma((3, 5)), dma((3, 5)),
+                dma((14,)), dma((3, 5)), dma((3, 5)),
                 dma((ng,)), dma((ng,)), dma((ns,)), dma((ns,)), dma((ng,)), dma((ng,)),
             ],
             compiler_params=pltpu.CompilerParams(
-                collective_id=0, has_side_effects=True, vmem_limit_bytes=48 << 20),
-        )(slabs(features), slabs(cotangent), w1, w2, w2t, first_bias.reshape(1, 32), second_bias.reshape(1, 32))
+                collective_id=0, has_side_effects=True, vmem_limit_bytes=32 << 20),
+        )(*(pltpu.with_memory_space_constraint(v, pltpu.MemorySpace.HBM) for v in (
+            features[0], cotangent[0], w1, w2, first_bias.reshape(1, 32), second_bias.reshape(1, 32))))
+        output, g1, gb1, g2, gb2 = pl.pallas_call(
+            functools.partial(unpack, rows),
+            out_shape=(
+                jax.ShapeDtypeStruct((32, 5, 8, LANES), BF),
+                jax.ShapeDtypeStruct((27, 32, 32), F32),
+                jax.ShapeDtypeStruct((1, 32), F32),
+                jax.ShapeDtypeStruct((27, 32, 32), F32),
+                jax.ShapeDtypeStruct((1, 32), F32),
+            ),
+            in_specs=[vm] * 2,
+            out_specs=(hbm, vm, vm, vm, vm),
+            scratch_shapes=[pltpu.VMEM((PAY, LANES), F32), dma((5,))],
+            compiler_params=pltpu.CompilerParams(vmem_limit_bytes=16 << 20),
+        )(gathered, mid.reshape(5, 32, 8, LANES))
         back = lambda g: g.reshape(3, 3, 3, 32, 32).transpose(3, 0, 1, 2, 4)
-        output = out.reshape(5, 8, 32, LANES).transpose(2, 0, 1, 3)[None]
-        return output, back(g1), gb1.reshape(32), back(g2), gb2.reshape(32)
+        return output[None], back(g1), gb1.reshape(32), back(g2), gb2.reshape(32)
 
     block = P("smp", None, "gx", None, "gz")
     return jax.shard_map(

time: 49.4 us -> 38.3 us (0.78)
  local copies, waits for them, and re-layouts: 6.52 us -> 0 us
  Pallas kernels: 42 us -> 37.5 us
    pallas_call x1, Pallas kernels: 42 us -> 35.7 us  [shards(): pl.pallas_call(functools.partial(kernel, sizes, cells ** (-0.5)), out_sha...]
    unnamed x16 -> x0, local copies, waits for them, and re-layouts: 4.43 us -> none
    pallas_call x0 -> x1, Pallas kernels: none -> 1.79 us  [shards(): pl.pallas_call(functools.partial(unpack, rows), out_shape=(jax.ShapeDtype...]
    transpose x3 -> x0, local copies, waits for them, and re-layouts: 1.23 us -> none  [the longest x1 1.13 us: shards(): w2t = second_weight.transpose(1, 2, 3, 4, 0).reshape(27, 32, 32)]
    reshape x1 -> x0, local copies, waits for them, and re-layouts: 0.85 us -> none  [shards(): output = out.reshape(5, 8, 32, LANES).transpose(2, 0, 1, 3)[None]]
where the time goes in v2:
time: 38.3 us; the launch traced here: 38.1 us
  Pallas kernels  37.5 us (98%)
  between operations  0.64 us (2%)
    pallas_call x1, Pallas kernels, shards(): pl.pallas_call(functools.partial(kernel, sizes, cells ** (-0.5)), out_sha...  35.7 us
    pallas_call x1, Pallas kernels, shards(): pl.pallas_call(functools.partial(unpack, rows), out_shape=(jax.ShapeDtype...  1.79 us

profile of v2, /device:TPU:1, one launch (start us, length us, event | category | flops | bytes accessed | tf_op | source)
XLA Modules:
  0.0 38.1 jit_solution(2671744752476292685)
XLA Ops:
  0.6 35.7 %shard_map.101 = (bf16[16,40,128]{2,1,0:T(8,128)(2,1)S(1)}, bf16[5,256,128]{2,1,0:T(8,128)(2,1)S(1)}) custom-call(bf16[32,5,8,128]{3,2,1,0:T(8,128)(2,1)} %bitcast.21, bf16[32,5,8,128]{3,2,1,0:T(8,128)(2,1)} %bitcast.22, bf16[27,32,32]{2,1,0:T(8,128)(2,1)} %bitcast.23, bf16[27,32,32]{2,1,0:T(8,128)(2,1)} %bitcast.24, f32[1,32]{1,0:T(1,128)} %bitcast.25, ...), custom_call_target="tpu_custom_call" | custom-call | tf_op jit(solution)/shard_map/pallas_call | solution.py:414
  36.3 1.8 %shard_map.102 = (bf16[32,5,8,128]{3,2,1,0:T(8,128)(2,1)}, f32[27,32,32]{2,1,0:T(8,128)}, f32[1,32]{1,0:T(1,128)}, f32[27,32,32]{2,1,0:T(8,128)}, f32[1,32]{1,0:T(1,128)}) custom-call(bf16[16,40,128]{2,1,0:T(8,128)(2,1)S(1)} %get-tuple-element.12.rc, bf16[5,32,8,128]{3,2,1,0:T(8,128)(2,1)S(1)} %bitcast.20), custom_call_target="tpu_custom_call" | custom-call | tf_op jit(solution)/shard_map/pallas_call | solution.py:455

commit v3 on v2

--- a/solution.py
+++ b/solution.py
@@ -11,30 +11,42 @@
 BF = jnp.bfloat16
 F32 = jnp.float32
 LANES = 128
-PAY = 640
+PAY = 448
 
 
 def kernel(sizes, scale, feat, cot, w1h, w2h, b1h, b2h, rc, out,
            vf, vc, w1, w2, b1, b2, pm, pe, ps,
-           sf, sc, sh, eo, ei, wa, wb, wv, dd, pg, pay, snd, ra, mid, rb, fin,
+           sf, sc, sh, eo, ei, wa, wb, wv, dd, pg, pay, pk, snd, ra, mid, rb, fin,
            ins, hs, hr, as_, ar, bs, br, cs, cr):
     ns, nx, nz = sizes
-    ng = nx * nz
-    rows = PAY // ng
+    hx = min(4, nx)
+    nlo = nx // hx
+    nzt, ny = nz * nlo, ns // 2
+    nr, na = 2 * hx, ny * nzt
+    rows = PAY // nr
     smp, gx, gz = lax.axis_index("smp"), lax.axis_index("gx"), lax.axis_index("gz")
-    me = gx * nz + gz
     left, right = lax.rem(gx + nx - 1, nx), lax.rem(gx + 1, nx)
     other = 1 - gz
+    x_at, z_at = lax.rem(gx, hx), gz * nlo + gx // hx
+    y_at, c_at = smp // 2, lax.rem(smp, 2)
     lane = lax.broadcasted_iota(jnp.int32, (32, LANES), 1)
     level = lax.rem(lane // 2, 8)
 
-    def in_group(d):
-        peer = lax.rem(me + d, ng)
-        return peer, (smp, peer // nz, lax.rem(peer, nz))
-
-    def in_samples(d):
-        peer = lax.rem(smp + d, ns)
-        return peer, (peer, gx, gz)
+    def device(x, y, z, c):
+        return (y * 2 + c, lax.rem(z, nlo) * hx + x, z // nlo)
+
+    def far(n, m):
+        return [(i, j) for i in range(n) for j in range(m) if i or j]
+
+    me_r, me_a = x_at * 2 + c_at, y_at * nzt + z_at
+    peers_r, peers_a = [], []
+    for i, j in sorted(far(hx, 2), key=lambda o: -2 * min(o[0], hx - o[0]) - o[1]):
+        x, c = lax.rem(x_at + i, hx), lax.rem(c_at + j, 2)
+        peers_r.append((x * 2 + c, device(x, y_at, z_at, c)))
+    for i, j in sorted(far(ny, nzt), key=lambda o: -min(o[0], ny - o[0]) - min(o[1], nzt - o[1])):
+        y, z = lax.rem(y_at + i, ny), lax.rem(z_at + j, nzt)
+        peers_a.append((y * nzt + z, device(x_at, y, z, c_at)))
+    near = ((smp, gx, other), (smp, left, other), (smp, right, other), (smp, left, gz), (smp, right, gz))
 
     load_f = [pltpu.make_async_copy(feat.at[:, x], vf.at[x], ins.at[x]) for x in range(5)]
     load_c = [pltpu.make_async_copy(cot.at[:, x], vc.at[x], ins.at[5 + x]) for x in range(5)]
@@ -46,14 +58,9 @@
         m.start()
 
     barrier = pltpu.get_barrier_semaphore()
-
-    @pl.loop(1, ng)
-    def _(d):
-        pl.semaphore_signal(barrier, inc=1, device_id=in_group(d)[1], device_id_type=MESH)
-
-    @pl.loop(1, ns)
-    def _(d):
-        pl.semaphore_signal(barrier, inc=1, device_id=in_samples(d)[1], device_id_type=MESH)
+    known = [dev for _, dev in peers_r] + [dev for _, dev in peers_a] + list(near)
+    for dev in known:
+        pl.semaphore_signal(barrier, inc=1, device_id=dev, device_id_type=MESH)
 
     def grid(height, width):
         return (lax.broadcasted_iota(jnp.int32, (height, width), 0),
@@ -62,7 +69,7 @@
     def hot(cond):
         return jnp.where(cond, 1.0, 0.0).astype(BF)
 
-    def constants():
+    def first_constants():
         r, c = grid(256, 256)
         pm[...] = hot((r // 32 == lax.rem(c, 8)) & (lax.rem(r, 32) == c // 8))
         r, c = grid(LANES, LANES)
@@ -70,12 +77,14 @@
         for x in range(5):
             pe[x * LANES:(x + 1) * LANES] = hot(
                 (c // 16 == x) & (((r == LANES - 1) & (side == 0)) | ((r == 0) & (side == 1))))
+
+    def later_constants():
         r, c = grid(LANES, 256)
-        near = hot(((c < LANES) & (c == r + 1)) | ((c >= LANES) & (c == r + LANES - 1)))
+        beside = hot(((c < LANES) & (c == r + 1)) | ((c >= LANES) & (c == r + LANES - 1)))
         r2 = lax.rem(r, 2)
         ends = ((r2 == 0) & (c == 0)) | ((r2 == 1) & (c == 255))
         for x in range(5):
-            ps[x, 0:LANES] = near
+            ps[x, 0:LANES] = beside
             ps[x, LANES:256] = hot((r // 16 == x) & ends)
 
     def rows_in(s, v):
@@ -94,11 +103,11 @@
 
     def halo(s, f):
         plan = (
-            (2, eo.at[f], ei.at[f, 1], (smp, gx, other)),
-            (3, eo.at[f], ei.at[f, 2], (smp, left, other)),
-            (4, eo.at[f], ei.at[f, 0], (smp, right, other)),
-            (0, s.at[1, 1], s.at[1, 6], (smp, left, gz)),
-            (1, s.at[1, 5], s.at[1, 0], (smp, right, gz)),
+            (2, eo.at[f], ei.at[f, 1], near[0]),
+            (3, eo.at[f], ei.at[f, 2], near[1]),
+            (4, eo.at[f], ei.at[f, 0], near[2]),
+            (0, s.at[1, 1], s.at[1, 6], near[3]),
+            (1, s.at[1, 5], s.at[1, 0], near[4]),
         )
         return [
             pltpu.make_async_remote_copy(
@@ -173,22 +182,21 @@
             return [tall[b * 32:(b + 1) * 32] for b in range(3)]
         return tap
 
-    constants()
+    first_constants()
     for m in load_f:
         m.wait()
     rows_in(sf, vf)
     edges(sf, 0)
-    pl.semaphore_wait(barrier, ng + ns - 2)
-    moves_f = halo(sf, 0)
-    for m in moves_f:
-        m.start()
     for m in load_c:
         m.wait()
     rows_in(sc, vc)
     edges(sc, 1)
+    pl.semaphore_wait(barrier, len(known))
+    moves_f = halo(sf, 0)
     moves_c = halo(sc, 1)
-    for m in moves_c:
-        m.start()
+    for m in moves_f[:3] + moves_c[:3] + moves_f[3:] + moves_c[3:]:
+        m.start()
+    later_constants()
     for m in load_w:
         m.wait()
 
@@ -211,8 +219,8 @@
         both = v + pltpu.roll(v, LANES - 2, 1)
         high = both.astype(BF).astype(F32)
         lanes = lax.broadcasted_iota(jnp.int32, v.shape, 1)
-        pair = jnp.where(lanes < 2, high, pltpu.roll(both - high, 2, 1))
-        return jnp.where(which & (lanes < 4), pair, v).astype(BF)
+        pair = jnp.where(lanes < 98, high, pltpu.roll(both - high, 2, 1))
+        return jnp.where(which & (lanes >= 96) & (lanes < 100), pair, v).astype(BF)
 
     for m in moves_f:
         m.wait_recv()
@@ -258,123 +266,81 @@
         own = jnp.concatenate([sh[1, 1 + x] for x in range(5)], axis=1)
         pay[288 + k * 32:288 + (k + 1) * 32] = diagonal(nt(spans(sc, 2 - c, 2 - a), own))
 
-    pay[576:608] = jnp.where(lane == 0, folded(sums), jnp.where(lane == 1, csum, 0.0))
-    pay[608:640] = jnp.zeros((32, LANES), F32)
+    biases = jnp.where(lane == 96, folded(sums), jnp.where(lane == 97, csum, 0.0))
+    for n in range(14):
+        g, j = n // 3, n % 3
+        if n < 12:
+            extra = pltpu.roll(pay[(4 * g + 3) * 32:(4 * g + 4) * 32], 96 - 32 * j, 1)
+            part = jnp.where(lane < 96, pay[(4 * g + j) * 32:(4 * g + j + 1) * 32], extra)
+        else:
+            part = pay[(n + 4) * 32:(n + 5) * 32]
+            if n == 13:
+                part = part + biases
+        pk[n * 32:(n + 1) * 32] = part
 
     def bias_rows(first):
         r = lax.broadcasted_iota(jnp.int32, (rows, LANES), 0) + first
-        return (r >= 576) & (r < 608)
-
-    for s in range(ng):
-        part = pay[s * rows:(s + 1) * rows]
-        if (s + 1) * rows > 576 and s * rows < 608:
-            snd[s] = split(part, bias_rows(s * rows))
-        else:
-            snd[s] = part.astype(BF)
-
-    def send_a(d):
-        peer, dev = in_group(d)
+        return r >= PAY - 32
+
+    for s in range(nr):
+        part = pk[s * rows:(s + 1) * rows]
+        snd[s] = split(part, bias_rows(s * rows)) if (s + 1) * rows > PAY - 32 else part.astype(BF)
+
+    def remote(src, dst, send, recv, dev):
         return pltpu.make_async_remote_copy(
-            src_ref=snd.at[peer], dst_ref=ra.at[me], send_sem=as_.at[peer], recv_sem=ar.at[me],
-            device_id=dev, device_id_type=MESH)
-
-    def from_a(d):
-        peer, dev = in_group(d)
-        return pltpu.make_async_remote_copy(
-            src_ref=snd.at[peer], dst_ref=ra.at[peer], send_sem=as_.at[peer], recv_sem=ar.at[peer],
-            device_id=dev, device_id_type=MESH)
-
-    @pl.loop(1, ng)
-    def _(d):
-        send_a(d).start()
-
-    ra[me] = snd[me]
+            src_ref=src, dst_ref=dst, send_sem=send, recv_sem=recv, device_id=dev, device_id_type=MESH)
+
+    out_a = [remote(snd.at[p], ra.at[me_r], as_.at[p], ar.at[me_r], dev) for p, dev in peers_r]
+    in_a = [remote(snd.at[p], ra.at[p], as_.at[p], ar.at[p], dev) for p, dev in peers_r]
+    out_b = [remote(mid, rb.at[me_a], bs.at[p], br.at[me_a], dev) for p, dev in peers_a]
+    in_b = [remote(mid, rb.at[p], bs.at[p], br.at[p], dev) for p, dev in peers_a]
+    out_c = [remote(fin, rc.at[me_r], cs.at[p], cr.at[me_r], dev) for p, dev in peers_r]
+    in_c = [remote(fin, rc.at[p], cs.at[p], cr.at[p], dev) for p, dev in peers_r]
+
+    for m in out_a:
+        m.start()
+    ra[me_r] = snd[me_r]
+
+    def total(ref, n):
+        acc = ref[0].astype(F32)
+        for s in range(1, n):
+            acc = acc + ref[s].astype(F32)
+        return acc
 
     for m in moves_h:
         m.wait_recv()
     shift(sh, 2)
     bias2 = column(b2)
-    for xs in tiles:
+
+    def finish(xs):
         v = conv(wb, sh, xs) + bias2
         for i, x in enumerate(xs):
             r = (v[:, i * LANES:(i + 1) * LANES] + sf[1, 1 + x].astype(F32)).astype(BF)
             back = lax.dot_general(pm[...], r, (((0,), (0,)), ((), ())), preferred_element_type=F32)
             out[x] = back.astype(BF)
 
-    @pl.loop(1, ng)
-    def _(d):
-        from_a(d).wait_recv()
-
-    def total(ref, n):
-        acc = ref[0].astype(F32)
-        for s in range(1, n):
-            acc = acc + ref[s].astype(F32)
-        return acc
-
-    mine = bias_rows(me * rows)
-    mid[...] = split(total(ra, ng), mine)
-
-    def send_b(d):
-        peer, dev = in_samples(d)
-        return pltpu.make_async_remote_copy(
-            src_ref=mid, dst_ref=rb.at[smp], send_sem=bs.at[peer], recv_sem=br.at[smp],
-            device_id=dev, device_id_type=MESH)
-
-    def from_b(d):
-        peer, dev = in_samples(d)
-        return pltpu.make_async_remote_copy(
-            src_ref=mid, dst_ref=rb.at[peer], send_sem=bs.at[peer], recv_sem=br.at[peer],
-            device_id=dev, device_id_type=MESH)
-
-    @pl.loop(1, ns)
-    def _(d):
-        send_b(d).start()
-
-    rb[smp] = mid[...]
-
-    @pl.loop(1, ns)
-    def _(d):
-        from_b(d).wait_recv()
-
-    fin[...] = split(total(rb, ns) * scale, mine)
-
-    def send_c(d):
-        peer, dev = in_group(d)
-        return pltpu.make_async_remote_copy(
-            src_ref=fin, dst_ref=rc.at[me], send_sem=cs.at[peer], recv_sem=cr.at[me],
-            device_id=dev, device_id_type=MESH)
-
-    def from_c(d):
-        peer, dev = in_group(d)
-        return pltpu.make_async_remote_copy(
-            src_ref=fin, dst_ref=rc.at[peer], send_sem=cs.at[peer], recv_sem=cr.at[peer],
-            device_id=dev, device_id_type=MESH)
-
-    @pl.loop(1, ng)
-    def _(d):
-        send_c(d).start()
-
-    rc[me] = fin[...]
-
-    @pl.loop(1, ng)
-    def _(d):
-        from_c(d).wait_recv()
-
-    for m in moves_f + moves_c + moves_h:
+    finish(tiles[0])
+    for m in in_a:
+        m.wait_recv()
+    mine = bias_rows(me_r * rows)
+    mid[...] = split(total(ra, nr), mine)
+    for m in out_b:
+        m.start()
+    rb[me_a] = mid[...]
+    finish(tiles[1])
+    finish(tiles[2])
+    for m in in_b:
+        m.wait_recv()
+    fin[...] = split(total(rb, na) * scale, mine)
+    for m in out_c:
+        m.start()
+    rc[me_r] = fin[...]
+    for m in moves_f + moves_c + moves_h + out_a + out_b:
         m.wait_send()
-
-    @pl.loop(1, ng)
-    def _(d):
-        send_a(d).wait_send()
-
-    @pl.loop(1, ns)
-    def _(d):
-        send_b(d).wait_send()
-
-    @pl.loop(1, ng)
-    def _(d):
-        send_c(d).wait_send()
-
+    for m in in_c:
+        m.wait_recv()
+    for m in out_c:
+        m.wait_send()
 
 def unpack(rows, rc, mid, out, g1, gb1, g2, gb2, pay, sem):
     moves = [pltpu.make_async_copy(mid.at[x], out.at[:, x], sem.at[x]) for x in range(5)]
@@ -382,17 +348,22 @@
         m.start()
     for s in range(PAY // rows):
         pay[s * rows:(s + 1) * rows] = rc[s].astype(F32)
-    for base, ref in ((0, g1), (288, g2)):
-        for k in range(9):
-            a, c = k // 3, k % 3
-            blk = pay[base + k * 32:base + (k + 1) * 32]
-            for b in range(3):
-                ref[a * 9 + b * 3 + c] = blk[:, b * 32:(b + 1) * 32]
-    tail = pay[576:608]
+    for n in range(18):
+        ref, k = (g1, n) if n < 9 else (g2, n - 9)
+        a, c = k // 3, k % 3
+        for b in range(3):
+            if n >= 16:
+                block, place = n - 4, b
+            elif n % 4 == 3:
+                block, place = 3 * (n // 4) + b, 3
+            else:
+                block, place = 3 * (n // 4) + n % 4, b
+            ref[a * 9 + b * 3 + c] = pay[block * 32:(block + 1) * 32, place * 32:(place + 1) * 32]
+    tail = pay[PAY - 32:]
     tail = tail + pltpu.roll(tail, LANES - 2, 1)
     row = lax.broadcasted_iota(jnp.int32, (32, 32), 0)
     col = lax.broadcasted_iota(jnp.int32, (32, 32), 1)
-    for i, ref in ((0, gb1), (1, gb2)):
+    for i, ref in ((96, gb1), (97, gb2)):
         ref[...] = jnp.sum(jnp.where(row == col, tail[:, i:i + 1], 0.0), axis=0, keepdims=True)
     for m in moves:
         m.wait()
@@ -401,8 +372,9 @@
 def solution(mesh):
     sizes = tuple(mesh.shape[n] for n in ("smp", "gx", "gz"))
     ns, nx, nz = sizes
-    ng = nx * nz
-    rows = PAY // ng
+    hx = min(4, nx)
+    nr, na = 2 * hx, ns * nx * nz // (2 * hx)
+    rows = PAY // nr
 
     def shards(features, first_weight, first_bias, second_weight, second_bias, cotangent):
         cells = ns * nx * nz * 5 * 8 * LANES
@@ -414,7 +386,7 @@
         gathered, mid = pl.pallas_call(
             functools.partial(kernel, sizes, cells ** -0.5),
             out_shape=(
-                jax.ShapeDtypeStruct((ng, rows, LANES), BF),
+                jax.ShapeDtypeStruct((nr, rows, LANES), BF),
                 jax.ShapeDtypeStruct((5, 256, LANES), BF),
             ),
             in_specs=[hbm] * 6,
@@ -439,14 +411,15 @@
                 pltpu.VMEM((9, 256, 256), BF),
                 pltpu.VMEM((5, 256, LANES), F32),
                 pltpu.VMEM((5, 256, LANES), BF),
+                pltpu.VMEM((576, LANES), F32),
                 pltpu.VMEM((PAY, LANES), F32),
-                pltpu.VMEM((ng, rows, LANES), BF),
-                pltpu.VMEM((ng, rows, LANES), BF),
+                pltpu.VMEM((nr, rows, LANES), BF),
+                pltpu.VMEM((nr, rows, LANES), BF),
                 pltpu.VMEM((rows, LANES), BF),
-                pltpu.VMEM((ns, rows, LANES), BF),
+                pltpu.VMEM((na, rows, LANES), BF),
                 pltpu.VMEM((rows, LANES), BF),
                 dma((14,)), dma((3, 5)), dma((3, 5)),
-                dma((ng,)), dma((ng,)), dma((ns,)), dma((ns,)), dma((ng,)), dma((ng,)),
+                dma((nr,)), dma((nr,)), dma((na,)), dma((na,)), dma((nr,)), dma((nr,)),
             ],
             compiler_params=pltpu.CompilerParams(
                 collective_id=0, has_side_effects=True, vmem_limit_bytes=32 << 20),

time: 38.3 us -> 35.1 us (0.916)
  Pallas kernels: 37.5 us -> 34.4 us
    pallas_call x1, Pallas kernels: 35.7 us -> 32.6 us  [shards(): pl.pallas_call(functools.partial(kernel, sizes, cells ** (-0.5)), out_sha...]
where the time goes in v3:
time: 35.1 us; the launch traced here: 35 us
  Pallas kernels  34.4 us (98%)
  between operations  0.64 us (2%)
    pallas_call x1, Pallas kernels, shards(): pl.pallas_call(functools.partial(kernel, sizes, cells ** (-0.5)), out_sha...  32.6 us
    pallas_call x1, Pallas kernels, shards(): pl.pallas_call(functools.partial(unpack, rows), out_shape=(jax.ShapeDtype...  1.8 us

profile of v3, /device:TPU:1, one launch (start us, length us, event | category | flops | bytes accessed | tf_op | source)
XLA Modules:
  0.0 35.0 jit_solution(16747557916262351137)
XLA Ops:
  0.6 32.6 %shard_map.101 = (bf16[8,56,128]{2,1,0:T(8,128)(2,1)S(1)}, bf16[5,256,128]{2,1,0:T(8,128)(2,1)S(1)}) custom-call(bf16[32,5,8,128]{3,2,1,0:T(8,128)(2,1)} %bitcast.21, bf16[32,5,8,128]{3,2,1,0:T(8,128)(2,1)} %bitcast.22, bf16[27,32,32]{2,1,0:T(8,128)(2,1)} %bitcast.23, bf16[27,32,32]{2,1,0:T(8,128)(2,1)} %bitcast.24, f32[1,32]{1,0:T(1,128)} %bitcast.25, ...), custom_call_target="tpu_custom_call" | custom-call | tf_op jit(solution)/shard_map/pallas_call | solution.py:386
  33.2 1.8 %shard_map.102 = (bf16[32,5,8,128]{3,2,1,0:T(8,128)(2,1)}, f32[27,32,32]{2,1,0:T(8,128)}, f32[1,32]{1,0:T(1,128)}, f32[27,32,32]{2,1,0:T(8,128)}, f32[1,32]{1,0:T(1,128)}) custom-call(bf16[8,56,128]{2,1,0:T(8,128)(2,1)S(1)} %get-tuple-element.12.rc, bf16[5,32,8,128]{3,2,1,0:T(8,128)(2,1)S(1)} %bitcast.20), custom_call_target="tpu_custom_call" | custom-call | tf_op jit(solution)/shard_map/pallas_call | solution.py:428

commit v4 on v3

--- a/solution.py
+++ b/solution.py
@@ -117,13 +117,14 @@
             for i, src, dst, dev in plan
         ]
 
-    def shift(s, f):
-        spread = []
-        for i in range(3):
-            e = ei[f, i].astype(F32)
-            spread.append(jnp.concatenate([jnp.where(level == y, e, 0.0) for y in range(8)], axis=0).astype(BF))
-        for slot in (1, 2, 3, 4, 5, 0, 6):
+    def shift(s, f, slots):
+        spread = {}
+        for slot in slots:
             which, x = (0, 4) if slot == 0 else (2, 0) if slot == 6 else (1, slot - 1)
+            if which not in spread:
+                e = ei[f, which].astype(F32)
+                spread[which] = jnp.concatenate(
+                    [jnp.where(level == y, e, 0.0) for y in range(8)], axis=0).astype(BF)
             wide = jnp.concatenate([s[1, slot], spread[which]], axis=1)
             moved = jnp.dot(wide, ps[x], preferred_element_type=F32).astype(BF)
             s[0, slot] = moved[:, :LANES]
@@ -202,7 +203,6 @@
 
     banded(wa, taps(w1))
     banded(wv, turned(w2))
-    banded(wb, taps(w2))
 
     def folded(v):
         total = v[0:32]
@@ -222,12 +222,11 @@
         pair = jnp.where(lanes < 98, high, pltpu.roll(both - high, 2, 1))
         return jnp.where(which & (lanes >= 96) & (lanes < 100), pair, v).astype(BF)
 
-    for m in moves_f:
-        m.wait_recv()
-    shift(sf, 0)
-    tiles = ((0, 1), (2, 3), (4,))
     bias = column(b1)
-    for xs in tiles:
+    inner, outer = (1, 2, 3, 4, 5), (0, 6)
+    tiles = ((1, 2), (3, 4), (0,))
+
+    def forward(xs):
         v = conv(wa, sf, xs) + bias
         q = 1.0 / (1.0 + jnp.exp(-v))
         h = (v * q).astype(BF)
@@ -235,21 +234,31 @@
         for i, x in enumerate(xs):
             sh[1, 1 + x] = h[:, i * LANES:(i + 1) * LANES]
             dd[x] = d[:, i * LANES:(i + 1) * LANES]
+
+    def backward(xs):
+        u = conv(wv, sc, xs)
+        part = jnp.zeros((256, LANES), F32)
+        for i, x in enumerate(xs):
+            p = (u[:, i * LANES:(i + 1) * LANES] * dd[x]).astype(BF)
+            pg[x] = p
+            part = part + p.astype(F32)
+        return part
+
+    for m in moves_f:
+        m.wait_recv()
+    shift(sf, 0, inner + outer)
+    for xs in tiles:
+        forward(xs)
     edges(sh, 2)
     moves_h = halo(sh, 2)
     for m in moves_h:
         m.start()
-
     for m in moves_c:
         m.wait_recv()
-    shift(sc, 1)
+    shift(sc, 1, inner + outer)
     sums = jnp.zeros((256, LANES), F32)
     for xs in tiles:
-        u = conv(wv, sc, xs)
-        for i, x in enumerate(xs):
-            p = (u[:, i * LANES:(i + 1) * LANES] * dd[x]).astype(BF)
-            pg[x] = p
-            sums = sums + p.astype(F32)
+        sums = sums + backward(xs)
 
     def spans(s, c, a):
         return jnp.concatenate([s[c, a + x] for x in range(5)], axis=1)
@@ -307,9 +316,7 @@
             acc = acc + ref[s].astype(F32)
         return acc
 
-    for m in moves_h:
-        m.wait_recv()
-    shift(sh, 2)
+    banded(wb, taps(w2))
     bias2 = column(b2)
 
     def finish(xs):
@@ -319,7 +326,6 @@
             back = lax.dot_general(pm[...], r, (((0,), (0,)), ((), ())), preferred_element_type=F32)
             out[x] = back.astype(BF)
 
-    finish(tiles[0])
     for m in in_a:
         m.wait_recv()
     mine = bias_rows(me_r * rows)
@@ -327,8 +333,11 @@
     for m in out_b:
         m.start()
     rb[me_a] = mid[...]
-    finish(tiles[1])
-    finish(tiles[2])
+    for m in moves_h:
+        m.wait_recv()
+    shift(sh, 2, inner + outer)
+    for xs in tiles:
+        finish(xs)
     for m in in_b:
         m.wait_recv()
     fin[...] = split(total(rb, na) * scale, mine)
@@ -342,14 +351,26 @@
     for m in out_c:
         m.wait_send()
 
-def unpack(rows, rc, mid, out, g1, gb1, g2, gb2, pay, sem):
+def unpack(rows, rc, mid, out, g1, gb1, g2, gb2, pay, v1, v2, vb, sem):
     moves = [pltpu.make_async_copy(mid.at[x], out.at[:, x], sem.at[x]) for x in range(5)]
     for m in moves:
         m.start()
     for s in range(PAY // rows):
         pay[s * rows:(s + 1) * rows] = rc[s].astype(F32)
+    tail = pay[PAY - 32:]
+    tail = tail + pltpu.roll(tail, LANES - 2, 1)
+    row = lax.broadcasted_iota(jnp.int32, (32, 32), 0)
+    col = lax.broadcasted_iota(jnp.int32, (32, 32), 1)
+
+    def send(src, dst):
+        moves.append(pltpu.make_async_copy(src, dst, sem.at[len(moves)]))
+        moves[-1].start()
+
+    for i, ref in enumerate((gb1, gb2)):
+        vb[i] = jnp.sum(jnp.where(row == col, tail[:, 96 + i:97 + i], 0.0), axis=0, keepdims=True)
+        send(vb.at[i], ref)
     for n in range(18):
-        ref, k = (g1, n) if n < 9 else (g2, n - 9)
+        ref, k = (v1, n) if n < 9 else (v2, n - 9)
         a, c = k // 3, k % 3
         for b in range(3):
             if n >= 16:
@@ -359,12 +380,9 @@
             else:
                 block, place = 3 * (n // 4) + n % 4, b
             ref[a * 9 + b * 3 + c] = pay[block * 32:(block + 1) * 32, place * 32:(place + 1) * 32]
-    tail = pay[PAY - 32:]
-    tail = tail + pltpu.roll(tail, LANES - 2, 1)
-    row = lax.broadcasted_iota(jnp.int32, (32, 32), 0)
-    col = lax.broadcasted_iota(jnp.int32, (32, 32), 1)
-    for i, ref in ((96, gb1), (97, gb2)):
-        ref[...] = jnp.sum(jnp.where(row == col, tail[:, i:i + 1], 0.0), axis=0, keepdims=True)
+        if c == 2:
+            part = pl.ds(a * 9, 9)
+            send(ref.at[part], (g1 if n < 9 else g2).at[part])
     for m in moves:
         m.wait()
 
@@ -435,8 +453,14 @@
                 jax.ShapeDtypeStruct((1, 32), F32),
             ),
             in_specs=[vm] * 2,
-            out_specs=(hbm, vm, vm, vm, vm),
-            scratch_shapes=[pltpu.VMEM((PAY, LANES), F32), dma((5,))],
+            out_specs=(hbm,) * 5,
+            scratch_shapes=[
+                pltpu.VMEM((PAY, LANES), F32),
+                pltpu.VMEM((27, 32, 32), F32),
+                pltpu.VMEM((27, 32, 32), F32),
+                pltpu.VMEM((2, 1, 32), F32),
+                dma((13,)),
+            ],
             compiler_params=pltpu.CompilerParams(vmem_limit_bytes=16 << 20),
         )(gathered, mid.reshape(5, 32, 8, LANES))
         back = lambda g: g.reshape(3, 3, 3, 32, 32).transpose(3, 0, 1, 2, 4)

time: 35.1 us -> 34.4 us (0.980)
  Pallas kernels: 34.4 us -> 33.6 us
    pallas_call x1, Pallas kernels: 1.8 us -> 1.18 us  [shards(): pl.pallas_call(functools.partial(unpack, rows), out_shape=(jax.ShapeDtype...]
where the time goes in v4:
time: 34.4 us; the launch traced here: 34.3 us
  Pallas kernels  33.6 us (98%)
  between operations  0.64 us (2%)
    pallas_call x1, Pallas kernels, shards(): pl.pallas_call(functools.partial(kernel, sizes, cells ** (-0.5)), out_sha...  32.5 us
    pallas_call x1, Pallas kernels, shards(): pl.pallas_call(functools.partial(unpack, rows), out_shape=(jax.ShapeDtype...  1.18 us

profile of v4, /device:TPU:1, one launch (start us, length us, event | category | flops | bytes accessed | tf_op | source)
XLA Modules:
  0.0 34.3 jit_solution(8937043057949758927)
XLA Ops:
  0.6 32.5 %shard_map.101 = (bf16[8,56,128]{2,1,0:T(8,128)(2,1)S(1)}, bf16[5,256,128]{2,1,0:T(8,128)(2,1)S(1)}) custom-call(bf16[32,5,8,128]{3,2,1,0:T(8,128)(2,1)} %bitcast.21, bf16[32,5,8,128]{3,2,1,0:T(8,128)(2,1)} %bitcast.22, bf16[27,32,32]{2,1,0:T(8,128)(2,1)} %bitcast.23, bf16[27,32,32]{2,1,0:T(8,128)(2,1)} %bitcast.24, f32[1,32]{1,0:T(1,128)} %bitcast.25, ...), custom_call_target="tpu_custom_call" | custom-call | tf_op jit(solution)/shard_map/pallas_call | solution.py:404
  33.1 1.2 %shard_map.102 = (bf16[32,5,8,128]{3,2,1,0:T(8,128)(2,1)}, f32[27,32,32]{2,1,0:T(8,128)}, f32[1,32]{1,0:T(1,128)}, f32[27,32,32]{2,1,0:T(8,128)}, f32[1,32]{1,0:T(1,128)}) custom-call(bf16[8,56,128]{2,1,0:T(8,128)(2,1)S(1)} %get-tuple-element.12.rc, bf16[5,32,8,128]{3,2,1,0:T(8,128)(2,1)S(1)} %bitcast.20), custom_call_target="tpu_custom_call" | custom-call | tf_op jit(solution)/shard_map/pallas_call | solution.py:446

commit v5 on v4

--- a/solution.py
+++ b/solution.py
@@ -22,7 +22,7 @@
     hx = min(4, nx)
     nlo = nx // hx
     nzt, ny = nz * nlo, ns // 2
-    nr, na = 2 * hx, ny * nzt
+    nr, na = 2 * ny, hx * nzt
     rows = PAY // nr
     smp, gx, gz = lax.axis_index("smp"), lax.axis_index("gx"), lax.axis_index("gz")
     left, right = lax.rem(gx + nx - 1, nx), lax.rem(gx + 1, nx)
@@ -38,14 +38,14 @@
     def far(n, m):
         return [(i, j) for i in range(n) for j in range(m) if i or j]
 
-    me_r, me_a = x_at * 2 + c_at, y_at * nzt + z_at
+    me_r, me_a = y_at * 2 + c_at, x_at * nzt + z_at
     peers_r, peers_a = [], []
-    for i, j in sorted(far(hx, 2), key=lambda o: -2 * min(o[0], hx - o[0]) - o[1]):
-        x, c = lax.rem(x_at + i, hx), lax.rem(c_at + j, 2)
-        peers_r.append((x * 2 + c, device(x, y_at, z_at, c)))
-    for i, j in sorted(far(ny, nzt), key=lambda o: -min(o[0], ny - o[0]) - min(o[1], nzt - o[1])):
-        y, z = lax.rem(y_at + i, ny), lax.rem(z_at + j, nzt)
-        peers_a.append((y * nzt + z, device(x_at, y, z, c_at)))
+    for i, j in sorted(far(ny, 2), key=lambda o: -2 * min(o[0], ny - o[0]) - o[1]):
+        u, c = lax.rem(y_at + i, ny), lax.rem(c_at + j, 2)
+        peers_r.append((u * 2 + c, device(x_at, u, z_at, c)))
+    for i, j in sorted(far(hx, nzt), key=lambda o: -min(o[0], hx - o[0]) - min(o[1], nzt - o[1])):
+        u, v = lax.rem(x_at + i, hx), lax.rem(z_at + j, nzt)
+        peers_a.append((u * nzt + v, device(u, y_at, v, c_at)))
     near = ((smp, gx, other), (smp, left, other), (smp, right, other), (smp, left, gz), (smp, right, gz))
 
     load_f = [pltpu.make_async_copy(feat.at[:, x], vf.at[x], ins.at[x]) for x in range(5)]
@@ -58,7 +58,7 @@
         m.start()
 
     barrier = pltpu.get_barrier_semaphore()
-    known = [dev for _, dev in peers_r] + [dev for _, dev in peers_a] + list(near)
+    known = [dev for _, dev in peers_r] + [dev for _, dev in peers_a]
     for dev in known:
         pl.semaphore_signal(barrier, inc=1, device_id=dev, device_id_type=MESH)
 
@@ -249,10 +249,6 @@
     shift(sf, 0, inner + outer)
     for xs in tiles:
         forward(xs)
-    edges(sh, 2)
-    moves_h = halo(sh, 2)
-    for m in moves_h:
-        m.start()
     for m in moves_c:
         m.wait_recv()
     shift(sc, 1, inner + outer)
@@ -260,6 +256,7 @@
     for xs in tiles:
         sums = sums + backward(xs)
 
+    found = {}
     def spans(s, c, a):
         return jnp.concatenate([s[c, a + x] for x in range(5)], axis=1)
 
@@ -269,20 +266,20 @@
     for k in range(9):
         a, c = k // 3, k % 3
         upstream = jnp.concatenate([pg[x] for x in range(5)], axis=1)
-        pay[k * 32:(k + 1) * 32] = diagonal(nt(upstream, spans(sf, c, a)))
+        found[k] = diagonal(nt(upstream, spans(sf, c, a)))
     for k in range(9):
         a, c = k // 3, k % 3
         own = jnp.concatenate([sh[1, 1 + x] for x in range(5)], axis=1)
-        pay[288 + k * 32:288 + (k + 1) * 32] = diagonal(nt(spans(sc, 2 - c, 2 - a), own))
+        found[9 + k] = diagonal(nt(spans(sc, 2 - c, 2 - a), own))
 
     biases = jnp.where(lane == 96, folded(sums), jnp.where(lane == 97, csum, 0.0))
     for n in range(14):
         g, j = n // 3, n % 3
         if n < 12:
-            extra = pltpu.roll(pay[(4 * g + 3) * 32:(4 * g + 4) * 32], 96 - 32 * j, 1)
-            part = jnp.where(lane < 96, pay[(4 * g + j) * 32:(4 * g + j + 1) * 32], extra)
+            extra = pltpu.roll(found[4 * g + 3], 96 - 32 * j, 1)
+            part = jnp.where(lane < 96, found[4 * g + j], extra)
         else:
-            part = pay[(n + 4) * 32:(n + 5) * 32]
+            part = found[n + 4]
             if n == 13:
                 part = part + biases
         pk[n * 32:(n + 1) * 32] = part
@@ -309,6 +306,10 @@
     for m in out_a:
         m.start()
     ra[me_r] = snd[me_r]
+    edges(sh, 2)
+    moves_h = halo(sh, 2)
+    for m in moves_h:
+        m.start()
 
     def total(ref, n):
         acc = ref[0].astype(F32)
@@ -390,8 +391,7 @@
 def solution(mesh):
     sizes = tuple(mesh.shape[n] for n in ("smp", "gx", "gz"))
     ns, nx, nz = sizes
-    hx = min(4, nx)
-    nr, na = 2 * hx, ns * nx * nz // (2 * hx)
+    nr, na = ns, nx * nz
     rows = PAY // nr
 
     def shards(features, first_weight, first_bias, second_weight, second_bias, cotangent):

time: 34.4 us -> 33.9 us (0.985)
  Pallas kernels: 33.6 us -> 33.1 us
    pallas_call x1, Pallas kernels: 32.5 us -> 31.9 us  [shards(): pl.pallas_call(functools.partial(kernel, sizes, cells ** (-0.5)), out_sha...]
where the time goes in v5:
time: 33.9 us; the launch traced here: 33.7 us
  Pallas kernels  33.1 us (98%)
  between operations  0.64 us (2%)
    pallas_call x1, Pallas kernels, shards(): pl.pallas_call(functools.partial(kernel, sizes, cells ** (-0.5)), out_sha...  31.9 us
    pallas_call x1, Pallas kernels, shards(): pl.pallas_call(functools.partial(unpack, rows), out_shape=(jax.ShapeDtype...  1.18 us

profile of v5, /device:TPU:1, one launch (start us, length us, event | category | flops | bytes accessed | tf_op | source)
XLA Modules:
  0.0 33.7 jit_solution(986211011686671216)
XLA Ops:
  0.6 31.9 %shard_map.101 = (bf16[8,56,128]{2,1,0:T(8,128)(2,1)S(1)}, bf16[5,256,128]{2,1,0:T(8,128)(2,1)S(1)}) custom-call(bf16[32,5,8,128]{3,2,1,0:T(8,128)(2,1)} %bitcast.21, bf16[32,5,8,128]{3,2,1,0:T(8,128)(2,1)} %bitcast.22, bf16[27,32,32]{2,1,0:T(8,128)(2,1)} %bitcast.23, bf16[27,32,32]{2,1,0:T(8,128)(2,1)} %bitcast.24, f32[1,32]{1,0:T(1,128)} %bitcast.25, ...), custom_call_target="tpu_custom_call" | custom-call | tf_op jit(solution)/shard_map/pallas_call | solution.py:404
  32.5 1.2 %shard_map.102 = (bf16[32,5,8,128]{3,2,1,0:T(8,128)(2,1)}, f32[27,32,32]{2,1,0:T(8,128)}, f32[1,32]{1,0:T(1,128)}, f32[27,32,32]{2,1,0:T(8,128)}, f32[1,32]{1,0:T(1,128)}) custom-call(bf16[8,56,128]{2,1,0:T(8,128)(2,1)S(1)} %get-tuple-element.12.rc, bf16[5,32,8,128]{3,2,1,0:T(8,128)(2,1)S(1)} %bitcast.20), custom_call_target="tpu_custom_call" | custom-call | tf_op jit(solution)/shard_map/pallas_call | solution.py:446

commit v6 on v5

--- a/solution.py
+++ b/solution.py
@@ -252,26 +252,26 @@
     for m in moves_c:
         m.wait_recv()
     shift(sc, 1, inner + outer)
+    found = {}
+    def spans(s, c, a):
+        return jnp.concatenate([s[c, a + x] for x in range(5)], axis=1)
+
+    def nt(p, r):
+        return lax.dot_general(p, r, (((1,), (1,)), ((), ())), preferred_element_type=F32)
+
+    for k in range(9):
+        a, c = k // 3, k % 3
+        own = jnp.concatenate([sh[1, 1 + x] for x in range(5)], axis=1)
+        found[9 + k] = diagonal(nt(spans(sc, 2 - c, 2 - a), own))
+
     sums = jnp.zeros((256, LANES), F32)
     for xs in tiles:
         sums = sums + backward(xs)
-
-    found = {}
-    def spans(s, c, a):
-        return jnp.concatenate([s[c, a + x] for x in range(5)], axis=1)
-
-    def nt(p, r):
-        return lax.dot_general(p, r, (((1,), (1,)), ((), ())), preferred_element_type=F32)
 
     for k in range(9):
         a, c = k // 3, k % 3
         upstream = jnp.concatenate([pg[x] for x in range(5)], axis=1)
         found[k] = diagonal(nt(upstream, spans(sf, c, a)))
-    for k in range(9):
-        a, c = k // 3, k % 3
-        own = jnp.concatenate([sh[1, 1 + x] for x in range(5)], axis=1)
-        found[9 + k] = diagonal(nt(spans(sc, 2 - c, 2 - a), own))
-
     biases = jnp.where(lane == 96, folded(sums), jnp.where(lane == 97, csum, 0.0))
     for n in range(14):
         g, j = n // 3, n % 3

time: 33.9 us -> 33.8 us (level)
  no operation moved by 1% of the time
where the time goes in v6:
time: 33.8 us; the launch traced here: 33.7 us
  Pallas kernels  33.1 us (98%)
  between operations  0.64 us (2%)
    pallas_call x1, Pallas kernels, shards(): pl.pallas_call(functools.partial(kernel, sizes, cells ** (-0.5)), out_sha...  31.9 us
    pallas_call x1, Pallas kernels, shards(): pl.pallas_call(functools.partial(unpack, rows), out_shape=(jax.ShapeDtype...  1.18 us

profile of v6, /device:TPU:1, one launch (start us, length us, event | category | flops | bytes accessed | tf_op | source)
XLA Modules:
  0.0 33.7 jit_solution(13413061256765225727)
XLA Ops:
  0.6 31.9 %shard_map.101 = (bf16[8,56,128]{2,1,0:T(8,128)(2,1)S(1)}, bf16[5,256,128]{2,1,0:T(8,128)(2,1)S(1)}) custom-call(bf16[32,5,8,128]{3,2,1,0:T(8,128)(2,1)} %bitcast.21, bf16[32,5,8,128]{3,2,1,0:T(8,128)(2,1)} %bitcast.22, bf16[27,32,32]{2,1,0:T(8,128)(2,1)} %bitcast.23, bf16[27,32,32]{2,1,0:T(8,128)(2,1)} %bitcast.24, f32[1,32]{1,0:T(1,128)} %bitcast.25, ...), custom_call_target="tpu_custom_call" | custom-call | tf_op jit(solution)/shard_map/pallas_call | solution.py:404
  32.5 1.2 %shard_map.102 = (bf16[32,5,8,128]{3,2,1,0:T(8,128)(2,1)}, f32[27,32,32]{2,1,0:T(8,128)}, f32[1,32]{1,0:T(1,128)}, f32[27,32,32]{2,1,0:T(8,128)}, f32[1,32]{1,0:T(1,128)}) custom-call(bf16[8,56,128]{2,1,0:T(8,128)(2,1)S(1)} %get-tuple-element.12.rc, bf16[5,32,8,128]{3,2,1,0:T(8,128)(2,1)S(1)} %bitcast.20), custom_call_target="tpu_custom_call" | custom-call | tf_op jit(solution)/shard_map/pallas_call | solution.py:446
